TPU v7x, 256 devices: a whole 4x4x8 slice. The times are simulated.
256 devices in a mesh: group: 8 (over y, x_lo), member: 32 (over x_hi, z, core).
Axes of the slice: x: 4 (x_hi: 2, x_lo: 2; x = x_hi * 2 + x_lo), y: 4, z: 8, core: 2. Of those that a mesh axis runs over, the one named last changes fastest.
Arguments:
- clips: bfloat16 [256, 14, 64, 640], P(('group', 'member')), may hold values from -4 to 4
- targets: bfloat16 [256, 14, 64, 640], P(('group', 'member')), may hold values from -6 to 6
- timestep: int32 [256], P(('group', 'member')), may hold values from 0 to 999
- identity: int32 [256], P(('group', 'member')), may hold values from 0 to 63
- conv1_weight: bfloat16 [1920, 640], P('member', 'group'), may hold values from -6 to 6
- conv2_weight: bfloat16 [1920, 640], P('member', 'group'), may hold values from -6 to 6
- rate1: bfloat16 [1920, 640], P('member', 'group'), may hold values from 0.029907227 to 0.29882812
- rate2: bfloat16 [1920, 640], P('member', 'group'), may hold values from 0.029907227 to 0.29882812
- time_proj: bfloat16 [1280, 640], replicated, may hold values from -0.15625 to 0.15625
- subject_table: float32 [64, 1280], replicated, may hold values from -6 to 6
Outputs:
- adapted_first: float32 [8, 1920, 640], P('group', 'member')
- adapted_second: float32 [8, 1920, 640], P('group', 'member')
All inputs are finite; a program needn't handle non-finite values.
Results may differ from a plain program's by a relative error of at most 0.0016.
Values may be sent and summed in bfloat16 or wider, within the bound.
A program may use at most 128 MiB of HBM per device.

v0:
```python
import math

import jax
import jax.numpy as jnp
from jax import lax
from jax.sharding import PartitionSpec as P

GN_GROUPS = 32


def time_bias(step_index, ident, subject_table, time_proj):
    half_width = subject_table.shape[1] // 2
    freqs = jnp.exp(-math.log(10000.0) * jnp.arange(half_width, dtype=jnp.float32) / half_width)
    angles = step_index.astype(jnp.float32) * freqs
    embedding = jnp.concatenate([jnp.cos(angles), jnp.sin(angles)])
    onehot = (jnp.arange(subject_table.shape[0], dtype=jnp.int32) == ident).astype(jnp.float32)
    embedding = embedding + jnp.dot(onehot, subject_table, precision=lax.Precision.HIGHEST)
    activated = jax.nn.silu(embedding).astype(jnp.bfloat16)
    return jnp.dot(activated[None, :], time_proj, preferred_element_type=jnp.float32)[0]


def group_norm(values):
    channels = values.shape[2]
    per_group = channels // GN_GROUPS
    counted = values.shape[0] * values.shape[1] * per_group

    def spread(sums):
        return jnp.repeat(sums.reshape(GN_GROUPS, per_group).sum(axis=1) / counted, per_group)

    centre = spread(values.sum(axis=(0, 1)))
    centred = values - centre
    variance = spread((centred * centred).sum(axis=(0, 1)))
    return centred * lax.rsqrt(variance + 1e-05)


def activate(values):
    return jax.nn.silu(group_norm(values))


def stack_taps(act_values):
    frames, points, channels = act_values.shape
    blank = jnp.zeros((1, points, channels), act_values.dtype)
    before = jnp.concatenate([blank, act_values[:-1]], axis=0)
    after = jnp.concatenate([act_values[1:], blank], axis=0)
    return jnp.concatenate([before, act_values, after], axis=2).reshape(
        frames * points, 3 * channels
    )


def fold_taps(grad_rows, frames, points, channels):
    shaped = grad_rows.reshape(frames, points, 3 * channels)
    blank = jnp.zeros((1, points, channels), jnp.float32)
    from_before = jnp.concatenate([shaped[1:, :, :channels], blank], axis=0)
    from_after = jnp.concatenate([blank, shaped[:-1, :, 2 * channels :]], axis=0)
    return shaped[:, :, channels : 2 * channels] + from_before + from_after


def fold_rows(stacked, portion):
    return jnp.dot(stacked, portion, preferred_element_type=jnp.float32)


def grad_terms(stacked, cotangent, weight_scale):
    product = lax.dot_general(
        stacked, cotangent, (((0,), (0,)), ((), ())), preferred_element_type=jnp.float32
    )
    return weight_scale * product


def shards(
    clips,
    targets,
    timestep,
    identity,
    conv1_weight,
    conv2_weight,
    rate1,
    rate2,
    time_proj,
    subject_table,
):
    frames, points, channels = (clips.shape[1], clips.shape[2], clips.shape[3])
    weight_scale = 1.0 / math.sqrt(3 * channels)
    latent = clips[0].astype(jnp.float32)
    bias_row = time_bias(timestep[0], identity[0], subject_table, time_proj)
    stacked_one = stack_taps(activate(latent).astype(jnp.bfloat16))
    contract_last = (((1,), (1,)), ((), ()))
    own_one, own_two, rate_one, rate_two = (
        lax.all_gather(conv1_weight, "group", axis=1, tiled=True),
        lax.all_gather(conv2_weight, "group", axis=1, tiled=True),
        lax.all_gather(rate1, "group", axis=1, tiled=True),
        lax.all_gather(rate2, "group", axis=1, tiled=True),
    )
    mixed_one = fold_rows(stacked_one, lax.all_gather(own_one, "member", axis=0, tiled=True))
    hidden = (weight_scale * mixed_one + bias_row).reshape(frames, points, channels)
    act_two, backward = jax.vjp(activate, hidden)
    stacked_two = stack_taps(act_two.astype(jnp.bfloat16))
    mixed_two = fold_rows(stacked_two, lax.all_gather(own_two, "member", axis=0, tiled=True))
    output = latent + (weight_scale * mixed_two).reshape(frames, points, channels)
    error = (
        (output - targets[0].astype(jnp.float32))
        .reshape(frames * points, channels)
        .astype(jnp.bfloat16)
    )
    grad_two = lax.psum_scatter(
        grad_terms(stacked_two, error, weight_scale), "member", scatter_dimension=0, tiled=True
    )
    back_rows = lax.dot_general(
        error,
        lax.all_gather(own_two, "member", axis=0, tiled=True),
        contract_last,
        preferred_element_type=jnp.float32,
    )
    grad_act = fold_taps(weight_scale * back_rows, frames, points, channels)
    grad_hidden = backward(grad_act)[0].reshape(frames * points, channels).astype(jnp.bfloat16)
    grad_one = lax.psum_scatter(
        grad_terms(stacked_one, grad_hidden, weight_scale),
        "member",
        scatter_dimension=0,
        tiled=True,
    )
    adapted_one = own_one.astype(jnp.float32) - rate_one.astype(jnp.float32) * grad_one
    adapted_two = own_two.astype(jnp.float32) - rate_two.astype(jnp.float32) * grad_two
    return (adapted_one[None], adapted_two[None])


def solution(mesh):
    return jax.shard_map(
        shards,
        mesh=mesh,
        in_specs=(
            P(("group", "member"), None, None, None),
            P(("group", "member"), None, None, None),
            P(("group", "member")),
            P(("group", "member")),
            P("member", "group"),
            P("member", "group"),
            P("member", "group"),
            P("member", "group"),
            P(),
            P(),
        ),
        out_specs=(P("group", "member", None), P("group", "member", None)),
        check_vma=False,
    )
```

profile of v0, /device:TPU:4, one launch (start us, length us, event | category | flops | bytes accessed | tf_op | source)
XLA Modules:
  0.0 360.7 jit_solution(12542882875444920755)
XLA Ops:
  7.3 29.0 %all-gather = bf16[8,80,60]{1,2,0:T(8,128)(2,1)S(1)} all-gather(bf16[1,80,60]{1,2,0:T(8,128)(2,1)} %bitcast.88), channel_id=1, replica_groups=mesh['group'=8,'member'=32] {'group'}, dimensions={0}, use_global_device_ids=true | all-gather | bytes 86400 | tf_op jit(solution)/shard_map/all_gather | solution.py:88
  36.2 0.1 copy.33
  36.3 0.8 reshape.98
  37.2 28.5 %all-gather.3 = bf16[8,80,60]{1,2,0:T(8,128)(2,1)S(1)} all-gather(bf16[1,80,60]{1,2,0:T(8,128)(2,1)} %bitcast.89), channel_id=1, replica_groups=mesh['group'=8,'member'=32] {'group'}, dimensions={0}, use_global_device_ids=true | all-gather | bytes 86400 | tf_op jit(solution)/shard_map/all_gather | solution.py:89
  65.8 0.8 reshape.104
  67.9 1.5 convert_reduce_fusion
  69.4 0.1 reshape.85
  69.5 0.2 convolution_reduce_fusion
  69.8 0.1 reduce_sum.121
  70.0 0.1 sub.39
  70.1 0.4 multiply_reduce_fusion.2
  70.5 0.1 reshape.86
  70.6 0.1 reduce_sum.123
  70.8 0.1 rsqrt.26
  70.9 28.6 %all-gather.1 = bf16[8,80,60]{1,2,0:T(8,128)(2,1)S(1)} all-gather(bf16[1,80,60]{1,2,0:T(8,128)(2,1)S(1)} %bitcast.90), channel_id=1, replica_groups=mesh['group'=8,'member'=32] {'group'}, dimensions={0}, use_global_device_ids=true | all-gather | bytes 86400 | tf_op jit(solution)/shard_map/all_gather | solution.py:90
  99.6 0.1 reshape.109
  99.8 28.4 %all-gather.5 = bf16[8,80,60]{1,2,0:T(8,128)(2,1)S(1)} all-gather(bf16[1,80,60]{1,2,0:T(8,128)(2,1)S(1)} %bitcast.91), channel_id=1, replica_groups=mesh['group'=8,'member'=32] {'group'}, dimensions={0}, use_global_device_ids=true | all-gather | bytes 86400 | tf_op jit(solution)/shard_map/all_gather | solution.py:91
  128.2 0.3 convolution_reduce_fusion.1
  128.6 0.7 multiply_convert_fusion.1
  129.3 0.3 fusion.32
  129.6 1.0 copy-done.4
  130.6 0.3 copy-done.5
  130.9 2.0 fusion.7
  132.9 4.2 %reshape.102 = bf16[1920,640]{1,0:T(8,128)(2,1)} reshape(bf16[32,60,640]{2,1,0:T(8,128)(2,1)} %all-gather.9.cloned.1.call-done) | data formatting | bytes 4915200
  137.1 7.1 %fusion.33 = (f32[640]{0:T(1024)S(1)}, f32[896,640]{1,0:T(8,128)}) fusion(f32[640]{0:T(1024)S(1)} %convolution_reduce_fusion.1, bf16[896,1920]{1,0:T(8,128)(2,1)} %bitcast.85, bf16[1920,640]{1,0:T(8,128)(2,1)} %reshape.102), kind=kOutput, calls=%fused_computation.65 | convolution fusion | flops 2203729408 | bytes 8197120 | tf_op jit(solution)/shard_map/dot_general | solution.py:59
  144.2 0.1 reshape.89
  144.2 0.1 reduce_sum.125
  144.4 0.1 sub.42
  144.6 1.9 multiply_reduce_fusion.1
  146.5 0.1 reshape.90
  146.6 0.1 reduce_sum.127
  146.8 0.1 rsqrt.28
  146.9 2.3 multiply_convert_fusion
  149.3 0.3 fusion.31
  149.6 1.9 fusion.9
  151.5 49.2 %all-gather.11.cloned.1.call-done = bf16[32,60,640]{2,1,0:T(8,128)(2,1)} async-done(((bf16[1,60,640]{2,1,0:T(8,128)(2,1)}), bf16[32,60,640]{2,1,0:T(8,128)(2,1)}) %all-gather.11.cloned.1.call-update) | async-done | bytes 2457616 | tf_op jit(solution)/shard_map/all_gather | solution.py:97
  200.7 4.1 %reshape.106 = bf16[1920,640]{1,0:T(8,128)(2,1)} reshape(bf16[32,60,640]{2,1,0:T(8,128)(2,1)} %all-gather.11.cloned.1.call-done) | data formatting | bytes 4915200
  204.8 6.4 %fusion.13 = bf16[896,640]{1,0:T(8,128)(2,1)S(1)} fusion(bf16[896,640]{1,0:T(8,128)(2,1)} %bitcast.92, bf16[1,14,64,640]{3,2,1,0:T(8,128)(2,1)} %param.10, bf16[896,1920]{1,0:T(8,128)(2,1)} %bitcast.83, bf16[1920,640]{1,0:T(8,128)(2,1)} %reshape.106), kind=kOutput, calls=%fused_computation.20 | convolution fusion | flops 2205450240 | bytes 9338880 | tf_op jit(solution)/shard_map/dot_general | solution.py:59
  211.3 3.0 convolution_multiply_fusion
  214.3 5.4 %convolution_multiply_fusion.1 = f32[1920,640]{1,0:T(8,128)} fusion(bf16[896,1920]{1,0:T(8,128)(2,1)S(1)} %bitcast.84, bf16[896,640]{1,0:T(8,128)(2,1)S(1)} %fusion.13), kind=kOutput, calls=%fused_computation.8 | convolution fusion | flops 2203238400 | bytes 9502720 | tf_op jit(solution)/shard_map/dot_general | solution.py:63
  219.7 0.5 fusion.30
  220.2 1.1 copy-done.1
  221.4 2.6 multiply_reduce_fusion
  223.9 0.1 reduce_sum.129
  224.0 0.2 multiply_reduce_fusion.3
  224.3 0.1 reshape.93
  224.4 2.8 fusion.15
  227.2 0.1 reduce_sum.132
  227.3 0.1 reduce_sum.133
  227.5 0.1 reshape.94
  227.6 8.6 %bitcast_multiply_fusion = f32[1920,640]{1,0:T(8,128)} fusion(f32[640]{0:T(1024)S(1)} %reshape.94, f32[14,64,640]{2,1,0:T(8,128)} %get-tuple-element.17, f32[14,64,640]{2,1,0:T(8,128)} %bitcast.79, f32[640]{0:T(1024)S(1)} %reshape.93, f32[640]{0:T(1024)S(1)} %rsqrt.28, f32[640]{0:T(1024)S(1)} %sub.42, bf16[13,64,640]{2,1,0:T(8,128)(2,1)} %copy-done.5, ...), kind=kOutput, calls=%fused_computation.6 | convolution fusion | flops 2224455680 | bytes 12789760 | tf_op jit(solution)/shard_map/dot_general | solution.py:63
  236.3 94.9 %fusion.28 = (f32[64,640]{1,0:T(8,128)S(1)}, f32[64,640]{1,0:T(8,128)S(1)}) fusion(f32[1920,640]{1,0:T(8,128)} %bitcast_multiply_fusion, f32[1920,640]{1,0:T(8,128)} %convolution_multiply_fusion.1), kind=kCustom, calls=%all-reduce-scatter.2 | all-reduce-scatter fusion | flops 2621441 | bytes 10159104
  331.3 2.1 collective-permute-start
  333.3 1.9 collective-permute-start.1
  335.3 0.1 reshape.110
  335.5 0.6 dynamic-slice.6
  336.7 1.9 collective-permute-start.2
  338.7 1.9 collective-permute-start.3
  340.6 4.7 %collective-permute-done.1 = f32[60,640]{1,0:T(8,128)S(1)} collective-permute-done((f32[60,640]{1,0:T(8,128)S(1)}, f32[60,640]{1,0:T(8,128)S(1)}, u32[]{:S(2)}, u32[]{:S(2)}) %collective-permute-start.1) | collective-permute-done | bytes 153632
  345.3 0.4 concatenate.36
  345.8 0.8 copy.37
  346.7 4.1 %collective-permute-done.3 = f32[60,640]{1,0:T(8,128)} collective-permute-done((f32[60,640]{1,0:T(8,128)S(1)}, f32[60,640]{1,0:T(8,128)}, u32[]{:S(2)}, u32[]{:S(2)}) %collective-permute-start.3) | collective-permute-done | bytes 153632
  350.8 2.2 concatenate.37
  353.0 0.8 copy.38
  (54 shorter events, 1.1 us)
Async XLA Ops:
  7.2 121.1 %copy-start = (bf16[1280,640]{1,0:T(8,128)(2,1)S(1)}, bf16[1280,640]{1,0:T(8,128)(2,1)}, u32[]{:S(2)}) copy-start(bf16[1280,640]{1,0:T(8,128)(2,1)} %param.18) | copy-start | bytes 4915204
  7.2 62.9 %copy-start.2 = (bf16[1,14,64,640]{3,2,1,0:T(8,128)(2,1)S(1)}, bf16[1,14,64,640]{3,2,1,0:T(8,128)(2,1)}, u32[]{:S(2)}) copy-start(bf16[1,14,64,640]{3,2,1,0:T(8,128)(2,1)} %param.10) | copy-start | bytes 3440644
  7.2 62.3 %copy-start.10 = (f32[64,1280]{1,0:T(8,128)S(1)}, f32[64,1280]{1,0:T(8,128)}, u32[]{:S(2)}) copy-start(f32[64,1280]{1,0:T(8,128)} %param.19) | copy-start | bytes 983044
  7.2 63.7 %copy-start.11 = (bf16[60,80]{1,0:T(8,128)(2,1)S(1)}, bf16[60,80]{1,0:T(8,128)(2,1)}, u32[]{:S(2)}) copy-start(bf16[60,80]{1,0:T(8,128)(2,1)} %param.16) | copy-start | bytes 28804
  7.2 125.7 %all-gather.9.cloned.1.call-start = ((), (), s32[]{:S(2)}) async-start(), calls=%async_computation | async-start | bytes 2703360 | tf_op jit(solution)/shard_map/all_gather | solution.py:93
  37.1 62.7 %copy-start.12 = (bf16[60,80]{1,0:T(8,128)(2,1)S(1)}, bf16[60,80]{1,0:T(8,128)(2,1)}, u32[]{:S(2)}) copy-start(bf16[60,80]{1,0:T(8,128)(2,1)} %param.17) | copy-start | bytes 28804
  37.1 163.6 %all-gather.11.cloned.1.call-start = ((), (), s32[]{:S(2)}) async-start(), calls=%async_computation.1 | async-start | bytes 2703360 | tf_op jit(solution)/shard_map/all_gather | solution.py:97
  99.8 28.8 %copy-start.3 = (bf16[1,14,64,640]{3,2,1,0:T(8,128)(2,1)S(1)}, bf16[1,14,64,640]{3,2,1,0:T(8,128)(2,1)}, u32[]{:S(2)}) copy-start(bf16[1,14,64,640]{3,2,1,0:T(8,128)(2,1)} %param.10) | copy-start | bytes 3440644
  129.5 1.0 copy-start.4
  129.6 1.3 copy-start.5
  204.8 6.4 %copy-start.7 = (bf16[1920,640]{1,0:T(8,128)(2,1)S(1)}, bf16[1920,640]{1,0:T(8,128)(2,1)}, u32[]{:S(2)}) copy-start(bf16[1920,640]{1,0:T(8,128)(2,1)} %reshape.106) | copy-start | bytes 7372804
  211.3 3.0 copy-start.6
  219.7 1.6 copy-start.1
  236.3 99.2 %copy-start.13 = (u32[256]{0:T(256)S(1)}, u32[256]{0:T(256)}, u32[]{:S(2)}) copy-start(u32[256]{0:T(256)} %constant.55) | copy-start | bytes 3076
  331.2 14.6 %copy-start.9 = (bf16[640,60]{0,1:T(8,128)(2,1)S(1)}, bf16[640,60]{0,1:T(8,128)(2,1)}, u32[]{:S(2)}) copy-start(bf16[640,60]{0,1:T(8,128)(2,1)} %reshape.98) | copy-start | bytes 230404
  331.2 21.8 %copy-start.8 = (bf16[640,60]{0,1:T(8,128)(2,1)S(1)}, bf16[640,60]{0,1:T(8,128)(2,1)}, u32[]{:S(2)}) copy-start(bf16[640,60]{0,1:T(8,128)(2,1)} %reshape.104) | copy-start | bytes 230404
  331.3 14.1 %collective-permute-start = (f32[64,640]{1,0:T(8,128)S(1)}, f32[64,640]{1,0:T(8,128)S(1)}, u32[]{:S(2)}, u32[]{:S(2)}) collective-permute-start(f32[64,640]{1,0:T(8,128)S(1)} %get-tuple-element.14), channel_id=1, source_target_pairs={{0,1},{1,2},{2,3},{3,4},{4,5},{5,6},{6,7},{7,8},{8,9},{9,10},{10,1... | collective-permute-start | bytes 491528
  333.3 12.0 %collective-permute-start.1 = (f32[60,640]{1,0:T(8,128)S(1)}, f32[60,640]{1,0:T(8,128)S(1)}, u32[]{:S(2)}, u32[]{:S(2)}) collective-permute-start(f32[60,640]{1,0:T(8,128)S(1)} %slice.35), channel_id=1, source_target_pairs={{0,2},{1,3},{2,4},{3,5},{4,6},{5,7},{6,8},{7,9},{8,10},{9,11},{10,... | collective-permute-start | bytes 460808
  336.7 14.0 %collective-permute-start.2 = (f32[64,640]{1,0:T(8,128)S(1)}, f32[64,640]{1,0:T(8,128)}, u32[]{:S(2)}, u32[]{:S(2)}) collective-permute-start(f32[64,640]{1,0:T(8,128)S(1)} %get-tuple-element.15), channel_id=1, source_target_pairs={{0,1},{1,2},{2,3},{3,4},{4,5},{5,6},{6,7},{7,8},{8,9},{9,10},{10,1... | collective-permute-start | bytes 491528
  338.7 12.1 %collective-permute-start.3 = (f32[60,640]{1,0:T(8,128)S(1)}, f32[60,640]{1,0:T(8,128)}, u32[]{:S(2)}, u32[]{:S(2)}) collective-permute-start(f32[60,640]{1,0:T(8,128)S(1)} %slice.36), channel_id=1, source_target_pairs={{0,2},{1,3},{2,4},{3,5},{4,6},{5,7},{6,8},{7,9},{8,10},{9,11},{10,... | collective-permute-start | bytes 460808
Sparse Core Ops, SparseCore 0:
  37.3 82.4 all-gather.8
  122.5 78.1 all-gather.10
where the time goes:
time: 361 us
  blocking collectives  210 us (58%)
  waiting for transfers between devices  58.1 us (16%)
  matrix products  31.1 us (9%)
  local copies, waits for them, and re-layouts  20.4 us (6%)
  other arithmetic  17.2 us (5%)
  between operations  16.5 us (5%)
  starting transfers between devices  7.9 us (2%)
    unnamed x1, blocking collectives  94.9 us
    all_gather x1, waiting for transfers between devices, shards(): lax.all_gather(own_two, 'member', axis=0, tiled=True)  49.2 us
    all_gather x1, blocking collectives, shards(): lax.all_gather(conv1_weight, 'group', axis=1, tiled=True)  29 us
    all_gather x1, blocking collectives, shards(): lax.all_gather(rate1, 'group', axis=1, tiled=True)  28.6 us
    all_gather x1, blocking collectives, shards(): lax.all_gather(conv2_weight, 'group', axis=1, tiled=True)  28.5 us
    all_gather x1, blocking collectives, shards(): lax.all_gather(rate2, 'group', axis=1, tiled=True)  28.4 us
    unnamed x39, local copies, waits for them, and re-layouts  17.2 us
    dot_general x2, matrix products, grad_terms(): lax.dot_general(stacked, cotangent, (((0,), (0,)), ((), ())), preferred_e...  14 us
  transfers between devices with their start and end apart: 6, of which 3 were waited for; matrix products, arithmetic and copies ran while one was open for 8% of the time, Pallas kernels for 0%

commit v1 on v0

--- a/solution.py
+++ b/solution.py
@@ -1,11 +1,314 @@
+import functools
 import math
 
 import jax
 import jax.numpy as jnp
 from jax import lax
+from jax.experimental import pallas as pl
+from jax.experimental.pallas import tpu as pltpu
 from jax.sharding import PartitionSpec as P
 
 GN_GROUPS = 32
+MESH = pl.DeviceIdType.MESH
+N_GROUP, N_MEMBER, NZ, NC, NX = 8, 32, 8, 2, 2
+ROWS, COLS, C = 60, 80, 640
+TAPS = 3 * C
+
+
+class Place:
+    def __init__(self):
+        self.g = lax.axis_index("group")
+        self.m = lax.axis_index("member")
+        self.core = lax.rem(self.m, 2)
+        self.q = lax.div(self.m, 2)
+        self.z = lax.rem(self.q, NZ)
+        self.xh = lax.div(self.q, NZ)
+        self.up = self.at(self.xh, self.zof(1), self.core)
+        self.down = self.at(self.xh, self.zof(-1), self.core)
+        self.across = self.at(1 - self.xh, self.z, self.core)
+        self.sibling = self.at(self.xh, self.z, 1 - self.core)
+
+    def at(self, xh, z, core):
+        return (self.g, (xh * NZ + z) * 2 + core)
+
+    def zof(self, step):
+        return lax.rem(self.z + (step + NZ), NZ)
+
+    def peer(self, step):
+        return lax.rem(self.g + step, N_GROUP)
+
+    def xof(self, piece):
+        return self.xh if piece == 0 else 1 - self.xh
+
+
+def remote(src, dst, send, recv, device):
+    return pltpu.make_async_remote_copy(
+        src_ref=src, dst_ref=dst, send_sem=send, recv_sem=recv, device_id=device, device_id_type=MESH
+    )
+
+
+def enter(place, with_group):
+    barrier = pltpu.get_barrier_semaphore()
+    partners = [place.up, place.down, place.across, place.sibling]
+    if with_group:
+        partners += [(place.peer(step), place.m) for step in range(1, N_GROUP)]
+    for partner in partners:
+        pl.semaphore_signal(barrier, inc=1, device_id=partner, device_id_type=MESH)
+    pl.semaphore_wait(barrier, len(partners))
+
+
+def gather_kernel(w1, w2, r1, r2, d1, d2, own_out, gbuf, wbuf, gsend, grecv, zsend, zrecv, xsend, xrecv, ssend, srecv):
+    place = Place()
+    for index, ref in enumerate((w1, w2, r1, r2)):
+        gbuf[index, place.g] = ref[...]
+    enter(place, True)
+    sends = []
+
+    def group_copy(part, step, here):
+        block = pl.ds(part, 1) if part < 2 else pl.ds(2, 2)
+        source = place.g if here else lax.rem(place.g + (N_GROUP - step), N_GROUP)
+        ref = gbuf.at[block, source]
+        return remote(ref, ref, gsend.at[part, step], grecv.at[part, step], (place.peer(step), place.m))
+
+    for part in range(3):
+        for step in range(1, N_GROUP):
+            copy = group_copy(part, step, True)
+            copy.start()
+            sends.append(copy)
+
+    def assemble(index):
+        blocks = [gbuf[index, group].astype(jnp.float32) for group in range(N_GROUP)]
+        return jnp.concatenate(blocks, axis=1).astype(jnp.bfloat16)
+
+    def slot(w, dist, piece):
+        return wbuf.at[w, place.xof(piece), place.zof(-dist), place.core]
+
+    def share(w, dist, piece):
+        ref = slot(w, dist, piece)
+        copy = remote(ref, ref, ssend.at[w, dist % NZ, piece], srecv.at[w, dist % NZ, piece], place.sibling)
+        copy.start()
+        sends.append(copy)
+
+    def hop(w, direction, dist, piece):
+        sign = 1 if direction == 0 else -1
+        ref = slot(w, sign * (dist - 1), piece)
+        to = place.up if direction == 0 else place.down
+        return remote(ref, ref, zsend.at[w, direction, dist, piece], zrecv.at[w, direction, dist, piece], to)
+
+    def hop_in(w, direction, dist, piece):
+        sign = 1 if direction == 0 else -1
+        ref = slot(w, sign * dist, piece)
+        to = place.up if direction == 0 else place.down
+        return remote(ref, ref, zsend.at[w, direction, dist, piece], zrecv.at[w, direction, dist, piece], to)
+
+    def exists(direction, dist, piece):
+        return dist < 4 or (dist == 4 and piece == direction)
+
+    def forward(w, direction, dist, piece):
+        if exists(direction, dist, piece):
+            copy = hop(w, direction, dist, piece)
+            copy.start()
+            sends.append(copy)
+
+    def ring(w):
+        for step in range(1, N_GROUP):
+            group_copy(w, step, False).wait_recv()
+        whole = assemble(w)
+        own_out[w] = whole
+        wbuf[w, place.xh, place.z, place.core] = whole
+        mine = slot(w, 0, 0)
+        copy = remote(mine, mine, xsend.at[w], xrecv.at[w], place.across)
+        copy.start()
+        sends.append(copy)
+        for direction in range(2):
+            forward(w, direction, 1, 0)
+        share(w, 0, 0)
+        yield
+        theirs = slot(w, 0, 1)
+        remote(theirs, theirs, xsend.at[w], xrecv.at[w], place.across).wait_recv()
+        for direction in range(2):
+            forward(w, direction, 1, 1)
+        share(w, 0, 1)
+        yield
+        for dist in range(1, 5):
+            for piece in range(2):
+                for direction in range(2):
+                    if exists(direction, dist, piece):
+                        hop_in(w, direction, dist, piece).wait_recv()
+                        forward(w, direction, dist + 1, piece)
+                        share(w, dist if direction == 0 else -dist, piece)
+                        yield
+        for dist in range(NZ):
+            for piece in range(2):
+                ref = wbuf.at[w, place.xof(piece), place.zof(-dist), 1 - place.core]
+                remote(ref, ref, ssend.at[w, dist, piece], srecv.at[w, dist, piece], place.sibling).wait_recv()
+        yield
+
+    def dense(w, out):
+        for m in range(N_MEMBER):
+            out[ROWS * m : ROWS * (m + 1), :] = wbuf[w, m // 16, (m // 2) % NZ, m % 2]
+
+    for _ in ring(0):
+        pass
+    dense(0, d1)
+    for _ in ring(1):
+        pass
+    dense(1, d2)
+    for step in range(1, N_GROUP):
+        group_copy(2, step, False).wait_recv()
+    own_out[2] = assemble(2)
+    own_out[3] = assemble(3)
+    for copy in sends:
+        copy.wait_send()
+
+
+def gather(w1, w2, r1, r2):
+    bf16 = jnp.bfloat16
+    dma = pltpu.SemaphoreType.DMA
+    vmem = pl.BlockSpec(memory_space=pltpu.VMEM)
+    return pl.pallas_call(
+        gather_kernel,
+        out_shape=(
+            jax.ShapeDtypeStruct((TAPS, C), bf16),
+            jax.ShapeDtypeStruct((TAPS, C), bf16),
+            jax.ShapeDtypeStruct((4, ROWS, C), bf16),
+        ),
+        in_specs=[vmem] * 4,
+        out_specs=(vmem,) * 3,
+        scratch_shapes=[
+            pltpu.VMEM((4, N_GROUP, ROWS, COLS), bf16),
+            pltpu.VMEM((2, NX, NZ, NC, ROWS, C), bf16),
+            dma((3, N_GROUP)),
+            dma((3, N_GROUP)),
+            dma((2, 2, 5, 2)),
+            dma((2, 2, 5, 2)),
+            dma((2,)),
+            dma((2,)),
+            dma((2, NZ, 2)),
+            dma((2, NZ, 2)),
+        ],
+        compiler_params=pltpu.CompilerParams(
+            collective_id=0, has_side_effects=True, vmem_limit_bytes=48 << 20
+        ),
+        name="gather_weights",
+    )(w1, w2, r1, r2)
+
+
+def reduce_kernel(g1, g2, own, o1, o2, blocks, sib_out, sib_in, hop_out, hop_in, last_out, last_in, x_out, x_in,
+                  ssend, srecv, zsend, zrecv, xsend, xrecv):
+    place = Place()
+    enter(place, False)
+    sends = []
+    order = [4, 3, 5, 2, 6, 1, 7, 0]
+
+    def lay(w, grad):
+        for m in range(N_MEMBER):
+            blocks[w, m // 16, (m // 2) % NZ, m % 2] = grad[ROWS * m : ROWS * (m + 1), :]
+
+    def pair(w):
+        for dist in order:
+            for piece in range(2):
+                sib_out[w, dist, piece] = blocks[w, place.xof(piece), place.zof(dist), 1 - place.core].astype(sib_out.dtype)
+                copy = remote(sib_out.at[w, dist, piece], sib_in.at[w, dist, piece],
+                              ssend.at[w, dist, piece], srecv.at[w, dist, piece], place.sibling)
+                copy.start()
+                sends.append(copy)
+
+    def summed(w, dist, piece):
+        remote(sib_out.at[w, dist, piece], sib_in.at[w, dist, piece],
+               ssend.at[w, dist, piece], srecv.at[w, dist, piece], place.sibling).wait_recv()
+        return (blocks[w, place.xof(piece), place.zof(dist), place.core]
+                + sib_in[w, dist, piece].astype(jnp.float32))
+
+    def exists(direction, dist, piece):
+        return dist < 4 or (dist == 4 and piece == direction)
+
+    def hop(w, direction, dist, piece):
+        to = place.up if direction == 0 else place.down
+        if dist == 1:
+            src, dst = last_out.at[w, direction, piece], last_in.at[w, direction, piece]
+        else:
+            src, dst = hop_out.at[w, direction, dist - 2, piece], hop_in.at[w, direction, dist - 2, piece]
+        return src, dst, remote(src, dst, zsend.at[w, direction, dist, piece], zrecv.at[w, direction, dist, piece], to)
+
+    def scatter(w):
+        for dist in (4, 3, 2, 1):
+            for piece in range(2):
+                for direction in range(2):
+                    if not exists(direction, dist, piece):
+                        continue
+                    total = summed(w, dist if direction == 0 else NZ - dist, piece)
+                    if exists(direction, dist + 1, piece):
+                        _, arrived, copy = hop(w, direction, dist + 1, piece)
+                        copy.wait_recv()
+                        total = total + arrived[...].astype(jnp.float32)
+                    src, _, copy = hop(w, direction, dist, piece)
+                    src[...] = total.astype(src.dtype)
+                    copy.start()
+                    sends.append(copy)
+                    yield
+        def final(piece):
+            total = summed(w, 0, piece)
+            for direction in range(2):
+                _, arrived, copy = hop(w, direction, 1, piece)
+                copy.wait_recv()
+                total = total + arrived[...].astype(jnp.float32)
+            return total
+        x_out[w] = final(1)
+        copy = remote(x_out.at[w], x_in.at[w], xsend.at[w], xrecv.at[w], place.across)
+        copy.start()
+        sends.append(copy)
+        yield
+        total = final(0)
+        copy.wait_recv()
+        out = (o1, o2)[w]
+        out[...] = own[w].astype(jnp.float32) - own[2 + w].astype(jnp.float32) * (total + x_in[w])
+        yield
+
+    lay(1, g2)
+    pair(1)
+    lay(0, g1)
+    pair(0)
+    for _ in scatter(1):
+        pass
+    for _ in scatter(0):
+        pass
+    for copy in sends:
+        copy.wait_send()
+
+
+def reduce(grad1, grad2, own):
+    f32, bf16 = jnp.float32, jnp.bfloat16
+    dma = pltpu.SemaphoreType.DMA
+    vmem = pl.BlockSpec(memory_space=pltpu.VMEM)
+    block = (ROWS, C)
+    return pl.pallas_call(
+        reduce_kernel,
+        out_shape=(jax.ShapeDtypeStruct(block, f32),) * 2,
+        in_specs=[vmem] * 3,
+        out_specs=(vmem,) * 2,
+        scratch_shapes=[
+            pltpu.VMEM((2, NX, NZ, NC) + block, f32),
+            pltpu.VMEM((2, NZ, 2) + block, f32),
+            pltpu.VMEM((2, NZ, 2) + block, f32),
+            pltpu.VMEM((2, 2, 3, 2) + block, bf16),
+            pltpu.VMEM((2, 2, 3, 2) + block, bf16),
+            pltpu.VMEM((2, 2, 2) + block, f32),
+            pltpu.VMEM((2, 2, 2) + block, f32),
+            pltpu.VMEM((2,) + block, f32),
+            pltpu.VMEM((2,) + block, f32),
+            dma((2, NZ, 2)),
+            dma((2, NZ, 2)),
+            dma((2, 2, 5, 2)),
+            dma((2, 2, 5, 2)),
+            dma((2,)),
+            dma((2,)),
+        ],
+        compiler_params=pltpu.CompilerParams(
+            collective_id=1, has_side_effects=True, vmem_limit_bytes=56 << 20
+        ),
+        name="reduce_gradients",
+    )(grad1, grad2, own)
 
 
 def time_bias(step_index, ident, subject_table, time_proj):
@@ -84,42 +387,29 @@
     bias_row = time_bias(timestep[0], identity[0], subject_table, time_proj)
     stacked_one = stack_taps(activate(latent).astype(jnp.bfloat16))
     contract_last = (((1,), (1,)), ((), ()))
-    own_one, own_two, rate_one, rate_two = (
-        lax.all_gather(conv1_weight, "group", axis=1, tiled=True),
-        lax.all_gather(conv2_weight, "group", axis=1, tiled=True),
-        lax.all_gather(rate1, "group", axis=1, tiled=True),
-        lax.all_gather(rate2, "group", axis=1, tiled=True),
-    )
-    mixed_one = fold_rows(stacked_one, lax.all_gather(own_one, "member", axis=0, tiled=True))
+    full_one, full_two, own = gather(conv1_weight, conv2_weight, rate1, rate2)
+    mixed_one = fold_rows(stacked_one, full_one)
     hidden = (weight_scale * mixed_one + bias_row).reshape(frames, points, channels)
     act_two, backward = jax.vjp(activate, hidden)
     stacked_two = stack_taps(act_two.astype(jnp.bfloat16))
-    mixed_two = fold_rows(stacked_two, lax.all_gather(own_two, "member", axis=0, tiled=True))
+    mixed_two = fold_rows(stacked_two, full_two)
     output = latent + (weight_scale * mixed_two).reshape(frames, points, channels)
     error = (
         (output - targets[0].astype(jnp.float32))
         .reshape(frames * points, channels)
         .astype(jnp.bfloat16)
     )
-    grad_two = lax.psum_scatter(
-        grad_terms(stacked_two, error, weight_scale), "member", scatter_dimension=0, tiled=True
-    )
+    grad_two = grad_terms(stacked_two, error, weight_scale)
     back_rows = lax.dot_general(
         error,
-        lax.all_gather(own_two, "member", axis=0, tiled=True),
+        full_two,
         contract_last,
         preferred_element_type=jnp.float32,
     )
     grad_act = fold_taps(weight_scale * back_rows, frames, points, channels)
     grad_hidden = backward(grad_act)[0].reshape(frames * points, channels).astype(jnp.bfloat16)
-    grad_one = lax.psum_scatter(
-        grad_terms(stacked_one, grad_hidden, weight_scale),
-        "member",
-        scatter_dimension=0,
-        tiled=True,
-    )
-    adapted_one = own_one.astype(jnp.float32) - rate_one.astype(jnp.float32) * grad_one
-    adapted_two = own_two.astype(jnp.float32) - rate_two.astype(jnp.float32) * grad_two
+    grad_one = grad_terms(stacked_one, grad_hidden, weight_scale)
+    adapted_one, adapted_two = reduce(grad_one, grad_two, own)
     return (adapted_one[None], adapted_two[None])
 
 

time: 361 us -> 173 us (0.48)
  the two profiles are of different devices: /device:TPU:4 before, /device:TPU:8 now
where the time goes in v1:
time: 173 us; the launch traced here: 172 us
  Pallas kernels  119 us (69%)
  matrix products  26.1 us (15%)
  other arithmetic  14.2 us (8%)
  local copies, waits for them, and re-layouts  11 us (6%)
  between operations  2.48 us (1%)
    pallas_call x1, Pallas kernels, reduce(): pl.pallas_call(reduce_kernel, out_shape=(jax.ShapeDtypeStruct(block, f32)...  61.8 us
    pallas_call x1, Pallas kernels, gather(): pl.pallas_call(gather_kernel, out_shape=(jax.ShapeDtypeStruct((TAPS, C),...  56.8 us
    dot_general x2, matrix products, grad_terms(): lax.dot_general(stacked, cotangent, (((0,), (0,)), ((), ())), preferred_e...  14.2 us
    unnamed x38, local copies, waits for them, and re-layouts  8.28 us
    dot_general x2, matrix products, fold_rows(): return jnp.dot(stacked, portion, preferred_element_type=jnp.float32)  7.37 us

profile of v1, /device:TPU:8, one launch (start us, length us, event | category | flops | bytes accessed | tf_op | source)
XLA Modules:
  0.0 172.3 jit_solution(13104864425681363460)
XLA Ops:
  0.6 0.0 copy-start
  0.6 0.0 copy-start.9
  1.5 1.2 convolution_reduce_fusion
  3.4 0.0 copy-done
  3.5 0.3 convolution_reduce_fusion.1
  3.8 0.2 convert_reduce_fusion
  4.0 0.1 reshape.85
  4.1 0.1 reduce_sum.121
  4.3 0.1 broadcast_in_dim.36
  4.3 0.1 sub.33
  4.4 0.4 multiply_reduce_fusion.2
  4.8 0.1 reshape.86
  4.9 0.1 reduce_sum.123
  5.0 0.1 broadcast_in_dim.37
  5.1 0.1 rsqrt.26
  5.2 1.9 %multiply_convert_fusion.1 = bf16[14,64,640]{2,1,0:T(8,128)(2,1)S(1)} fusion(bf16[1,14,64,640]{3,2,1,0:T(8,128)(2,1)} %param.10, f32[640]{0:T(1024)S(1)} %rsqrt.26, f32[640]{0:T(1024)S(1)} %sub.33), kind=kLoop, calls=%fused_computation.29 | loop fusion | flops 4587520 | bytes 2298880 | tf_op jit(solution)/shard_map/convert_element_type | solution.py:388
  7.1 0.3 fusion.25
  7.4 0.0 copy-start.11
  7.5 0.0 copy-start.12
  7.5 0.0 copy-start.2
  7.5 0.0 copy-start.3
  7.5 0.0 copy-start.4
  7.5 0.0 copy-start.5
  7.5 0.5 fusion.5
  8.0 0.5 copy-done.11
  8.5 0.3 copy-done.12
  8.8 56.8 %gather_weights.1 = (bf16[1920,640]{1,0:T(8,128)(2,1)S(1)}, bf16[1920,640]{1,0:T(8,128)(2,1)S(1)}, bf16[4,60,640]{2,1,0:T(8,128)(2,1)S(1)}) custom-call(bf16[60,80]{1,0:T(8,128)(2,1)S(1)} %copy-done.2, bf16[60,80]{1,0:T(8,128)(2,1)S(1)} %copy-done.3, bf16[60,80]{1,0:T(8,128)(2,1)S(1)} %copy-done.4, bf16[60,80]{1,0:T(8,128)(2,1)S(1)} %copy-done.5), custom_call_target="tpu_custom_call" | custom-call | tf_op jit(solution)/shard_map/gather_weights/pallas_call | solution.py:169
  65.5 4.4 %fusion.26 = (f32[640]{0:T(1024)S(1)}, f32[896,640]{1,0:T(8,128)}) fusion(f32[640]{0:T(1024)S(1)} %convolution_reduce_fusion.1, bf16[896,1920]{1,0:T(8,128)(2,1)S(1)} %bitcast.45, bf16[1920,640]{1,0:T(8,128)(2,1)S(1)} %get-tuple-element.7), kind=kOutput, calls=%fused_computation.57 | convolution fusion | flops 2203729408 | bytes 8197120 | tf_op jit(solution)/shard_map/dot_general | solution.py:362
  69.9 0.1 reshape.89
  70.0 0.1 reduce_sum.125
  70.2 0.1 broadcast_in_dim.38
  70.2 0.1 sub.36
  70.4 1.9 %multiply_reduce_fusion.1 = f32[640]{0:T(1024)S(1)} fusion(f32[896,640]{1,0:T(8,128)} %get-tuple-element.27, f32[640]{0:T(1024)S(1)} %sub.36), kind=kLoop, calls=%fused_computation.27 | loop fusion | flops 1719680 | bytes 2298880 | tf_op jit(solution)/shard_map/jvp()/reduce_sum | solution.py:335
  72.3 0.1 reshape.90
  72.4 0.1 reduce_sum.127
  72.5 0.1 broadcast_in_dim.39
  72.6 0.1 rsqrt.28
  72.7 2.3 %multiply_convert_fusion = bf16[14,64,640]{2,1,0:T(8,128)(2,1)S(1)} fusion(f32[14,64,640]{2,1,0:T(8,128)} %bitcast.37, f32[640]{0:T(1024)S(1)} %rsqrt.28, f32[640]{0:T(1024)S(1)} %sub.36), kind=kLoop, calls=%fused_computation.25 | loop fusion | flops 4014080 | bytes 3445760 | tf_op jit(solution)/shard_map/convert_element_type | solution.py:394
  75.1 0.3 fusion.24
  75.3 0.0 copy-start.10
  75.4 0.0 copy-start.15
  75.4 0.7 fusion.7
  76.0 1.8 %copy-done.13 = bf16[14,64,1920]{2,1,0:T(8,128)(2,1)} copy-done((bf16[14,64,1920]{2,1,0:T(8,128)(2,1)}, bf16[14,64,1920]{2,1,0:T(8,128)(2,1)S(1)}, u32[]{:S(2)}) %copy-start.13) | copy-done | bytes 3440664
  77.8 0.5 copy-done.10
  78.3 0.7 copy-done.15
  78.9 3.0 %fusion.11 = bf16[896,640]{1,0:T(8,128)(2,1)S(1)} fusion(bf16[896,640]{1,0:T(8,128)(2,1)S(1)} %bitcast.48, bf16[1,14,64,640]{3,2,1,0:T(8,128)(2,1)S(1)} %copy-done.10, bf16[896,1920]{1,0:T(8,128)(2,1)S(1)} %bitcast.43, bf16[1920,640]{1,0:T(8,128)(2,1)S(1)} %copy-done.7), kind=kOutput, calls=%fused_computation.20 | convolution fusion | flops 2205450240 | bytes 9338880 | tf_op jit(solution)/shard_map/dot_general | solution.py:362
  81.9 3.0 %convolution_multiply_fusion = f32[896,1920]{1,0:T(8,128)S(1)} fusion(bf16[896,640]{1,0:T(8,128)(2,1)S(1)} %fusion.11, bf16[1920,640]{1,0:T(8,128)(2,1)S(1)} %copy-done.7), kind=kOutput, calls=%fused_computation.7 | convolution fusion | flops 2203729920 | bytes 10485760 | tf_op jit(solution)/shard_map/dot_general | solution.py:403
  84.9 0.5 fusion.23
  85.4 1.1 copy-done.8
  86.5 2.6 %multiply_reduce_fusion = (f32[640]{0:T(1024)S(1)}, f32[14,64,640]{2,1,0:T(8,128)}) fusion(f32[14,64,640]{2,1,0:T(8,128)S(1)} %bitcast.40, f32[640]{0:T(1024)S(1)} %sub.36, f32[640]{0:T(1024)S(1)} %rsqrt.28, f32[13,64,640]{2,1,0:T(8,128)S(1)} %get-tuple-element.19, f32[13,64,640]{2,1,0:T(8,128)S(1)} %get-tuple-element.18, f32[14,64,1920]{2,1,0:T(8,128)S(1)} %bitcast.42), kind=kLoop, calls=%fused_computation.24 | loop fusion | flops 8600960 | bytes 11148800 | tf_op jit(solution)/shard_map/transpose(jvp())/reduce_sum | solution.py:336
  89.1 0.1 reduce_sum.129
  89.2 0.2 multiply_reduce_fusion.3
  89.4 0.1 broadcast_in_dim.41
  89.5 0.1 reshape.93
  89.6 2.8 %fusion.13 = f32[640]{0:T(1024)S(1)} fusion(f32[640]{0:T(1024)S(1)} %reshape.93, f32[14,64,640]{2,1,0:T(8,128)} %bitcast.38, f32[640]{0:T(1024)S(1)} %sub.36, f32[14,64,640]{2,1,0:T(8,128)} %get-tuple-element.17, f32[640]{0:T(1024)S(1)} %rsqrt.28), kind=kLoop, calls=%fused_computation.35 | loop fusion | flops 3440000 | bytes 4597760 | tf_op jit(solution)/shard_map/transpose(jvp())/reduce_sum | solution.py:334
  92.4 0.1 reduce_sum.132
  92.5 0.1 reduce_sum.133
  92.7 0.1 broadcast_in_dim.43
  92.7 0.1 reshape.94
  92.9 8.5 %bitcast_multiply_fusion.g1 = f32[1920,640]{1,0:T(8,128)} fusion(f32[640]{0:T(1024)S(1)} %reshape.94, f32[14,64,640]{2,1,0:T(8,128)} %get-tuple-element.17, f32[14,64,640]{2,1,0:T(8,128)} %bitcast.39, f32[640]{0:T(1024)S(1)} %reshape.93, f32[640]{0:T(1024)S(1)} %rsqrt.28, f32[640]{0:T(1024)S(1)} %sub.36, bf16[13,64,640]{2,1,0:T(8,128)(2,1)} %copy-done.12, ...), kind=kOutput, calls=%fused_computation.6 | convolution fusion | flops 2224455680 | bytes 12789760 | tf_op jit(solution)/shard_map/dot_general | solution.py:366
  101.4 5.7 %convolution_multiply_fusion.1.g2 = f32[1920,640]{1,0:T(8,128)} fusion(bf16[896,1920]{1,0:T(8,128)(2,1)S(1)} %bitcast.44, bf16[896,640]{1,0:T(8,128)(2,1)S(1)} %copy-done.17), kind=kOutput, calls=%fused_computation.8 | convolution fusion | flops 2203238400 | bytes 9502720 | tf_op jit(solution)/shard_map/dot_general | solution.py:366
  107.1 61.8 %reduce_gradients.1 = (f32[60,640]{1,0:T(8,128)}, f32[60,640]{1,0:T(8,128)}) custom-call(f32[1920,640]{1,0:T(8,128)} %bitcast_multiply_fusion.g1, f32[1920,640]{1,0:T(8,128)} %convolution_multiply_fusion.1.g2, bf16[4,60,640]{2,1,0:T(8,128)(2,1)} %copy-done.1), custom_call_target="tpu_custom_call" | custom-call | tf_op jit(solution)/shard_map/reduce_gradients/pallas_call | solution.py:285
  168.9 1.7 %copy.14 = f32[1,60,640]{2,0,1:T(1,128)} copy(f32[1,60,640]{2,1,0:T(8,128)} %bitcast.47) | data formatting | bytes 307200
  170.6 1.7 %copy.15 = f32[1,60,640]{2,0,1:T(1,128)} copy(f32[1,60,640]{2,1,0:T(8,128)} %bitcast.46) | data formatting | bytes 307200
  (28 shorter events, 0.1 us)
Async XLA Ops:
  0.6 2.8 %copy-start = (bf16[1280,640]{1,0:T(8,128)(2,1)S(1)}, bf16[1280,640]{1,0:T(8,128)(2,1)}, u32[]{:S(2)}) copy-start(bf16[1280,640]{1,0:T(8,128)(2,1)} %param.18) | copy-start | bytes 4915204
  0.6 3.1 %copy-start.9 = (bf16[1,14,64,640]{3,2,1,0:T(8,128)(2,1)S(1)}, bf16[1,14,64,640]{3,2,1,0:T(8,128)(2,1)}, u32[]{:S(2)}) copy-start(bf16[1,14,64,640]{3,2,1,0:T(8,128)(2,1)} %param.10) | copy-start | bytes 3440644
  7.4 1.0 copy-start.11
  7.5 1.3 copy-start.12
  7.5 1.3 copy-start.2
  7.5 1.3 copy-start.3
  7.5 1.3 copy-start.4
  7.5 1.3 copy-start.5
  65.5 4.4 %copy-start.1 = (bf16[4,60,640]{2,1,0:T(8,128)(2,1)}, bf16[4,60,640]{2,1,0:T(8,128)(2,1)S(1)}, u32[]{:S(2)}) copy-start(bf16[4,60,640]{2,1,0:T(8,128)(2,1)S(1)} %get-tuple-element.9.own) | copy-start | bytes 921604
  65.5 4.4 %copy-start.6 = (bf16[1920,640]{1,0:T(8,128)(2,1)}, bf16[1920,640]{1,0:T(8,128)(2,1)S(1)}, u32[]{:S(2)}) copy-start(bf16[1920,640]{1,0:T(8,128)(2,1)S(1)} %get-tuple-element.8) | copy-start | bytes 7372804
  75.3 2.5 %copy-start.7 = (bf16[1920,640]{1,0:T(8,128)(2,1)S(1)}, bf16[1920,640]{1,0:T(8,128)(2,1)}, u32[]{:S(2)}) copy-start(bf16[1920,640]{1,0:T(8,128)(2,1)} %copy-done.6) | copy-start | bytes 7372804
  75.3 2.9 %copy-start.10 = (bf16[1,14,64,640]{3,2,1,0:T(8,128)(2,1)S(1)}, bf16[1,14,64,640]{3,2,1,0:T(8,128)(2,1)}, u32[]{:S(2)}) copy-start(bf16[1,14,64,640]{3,2,1,0:T(8,128)(2,1)} %param.10) | copy-start | bytes 3440644
  75.4 3.6 %copy-start.15 = (bf16[1,14,64,640]{3,2,1,0:T(8,128)(2,1)S(1)}, bf16[1,14,64,640]{3,2,1,0:T(8,128)(2,1)}, u32[]{:S(2)}) copy-start(bf16[1,14,64,640]{3,2,1,0:T(8,128)(2,1)} %param.11) | copy-start | bytes 3440644
  76.0 1.8 %copy-start.13 = (bf16[14,64,1920]{2,1,0:T(8,128)(2,1)}, bf16[14,64,1920]{2,1,0:T(8,128)(2,1)S(1)}, u32[]{:S(2)}) copy-start(bf16[14,64,1920]{2,1,0:T(8,128)(2,1)S(1)} %fusion.7) | copy-start | bytes 10321924
  81.9 3.0 %copy-start.16 = (bf16[896,640]{1,0:T(8,128)(2,1)}, bf16[896,640]{1,0:T(8,128)(2,1)S(1)}, u32[]{:S(2)}) copy-start(bf16[896,640]{1,0:T(8,128)(2,1)S(1)} %fusion.11) | copy-start | bytes 3440644
  84.9 1.6 copy-start.8
  92.8 8.6 %copy-start.14 = (bf16[14,64,1920]{2,1,0:T(8,128)(2,1)S(1)}, bf16[14,64,1920]{2,1,0:T(8,128)(2,1)}, u32[]{:S(2)}) copy-start(bf16[14,64,1920]{2,1,0:T(8,128)(2,1)} %copy-done.13) | copy-start | bytes 10321924
  92.8 8.5 %copy-start.17 = (bf16[896,640]{1,0:T(8,128)(2,1)S(1)}, bf16[896,640]{1,0:T(8,128)(2,1)}, u32[]{:S(2)}) copy-start(bf16[896,640]{1,0:T(8,128)(2,1)} %copy-done.16) | copy-start | bytes 3440644

commit v2 on v1

v2 whole, which is shorter than its diff:
```python
import functools
import math

import jax
import jax.numpy as jnp
from jax import lax
from jax.experimental import pallas as pl
from jax.experimental.pallas import tpu as pltpu
from jax.sharding import PartitionSpec as P

GN_GROUPS = 32
MESH = pl.DeviceIdType.MESH
N_GROUP, N_MEMBER, NZ, NC, NX = 8, 32, 8, 2, 2
ROWS, COLS, C = 60, 80, 640
TAPS = 3 * C
FRAMES, HW = 14, 64
POINTS = FRAMES * HW
PER_GROUP = C // GN_GROUPS
SCALE = 1.0 / math.sqrt(TAPS)
UNIT = 128


class Place:
    def __init__(self):
        self.g = lax.axis_index("group")
        self.m = lax.axis_index("member")
        self.core = lax.rem(self.m, 2)
        self.q = lax.div(self.m, 2)
        self.z = lax.rem(self.q, NZ)
        self.xh = lax.div(self.q, NZ)
        self.up = self.at(self.xh, self.zof(1), self.core)
        self.down = self.at(self.xh, self.zof(-1), self.core)
        self.across = self.at(1 - self.xh, self.z, self.core)
        self.sibling = self.at(self.xh, self.z, 1 - self.core)

    def at(self, xh, z, core):
        return (self.g, (xh * NZ + z) * 2 + core)

    def zof(self, step):
        return lax.rem(self.z + (step + NZ), NZ)

    def peer(self, step):
        return lax.rem(self.g + step, N_GROUP)

    def xof(self, piece):
        return self.xh if piece == 0 else 1 - self.xh


def remote(src, dst, send, recv, device):
    return pltpu.make_async_remote_copy(
        src_ref=src, dst_ref=dst, send_sem=send, recv_sem=recv, device_id=device, device_id_type=MESH
    )


def enter(place, with_group):
    barrier = pltpu.get_barrier_semaphore()
    partners = [place.up, place.down, place.across, place.sibling]
    if with_group:
        partners += [(place.peer(step), place.m) for step in range(1, N_GROUP)]
    for partner in partners:
        pl.semaphore_signal(barrier, inc=1, device_id=partner, device_id_type=MESH)
    pl.semaphore_wait(barrier, len(partners))


def exists(direction, dist, piece):
    return dist < 4 or (dist == 4 and piece == direction)


def step_kernel(
    clip_hbm, target_hbm, proj_hbm, embed, w1, w2, r1, r2, o1, o2,
    clip, target, proj, same_group, act_one, act_two, err, grad_hid, flip_one, flip_two, hid, weights, grad,
    gbuf, wbuf, own, blocks, sib_in, hop_out, hop_in, last_out, last_in, x_out, x_in,
    load_sem, gsend, grecv, zsend, zrecv, xsend, xrecv, ssend, srecv,
    rsend, rrecv, ysend, yrecv, psend, precv,
):
    f32, bf16 = jnp.float32, jnp.bfloat16
    place = Place()
    sends = []

    def go(copy):
        copy.start()
        sends.append(copy)

    loads = [
        pltpu.make_async_copy(src, dst, load_sem.at[i])
        for i, (src, dst) in enumerate(((clip_hbm, clip), (proj_hbm, proj), (target_hbm, target)))
    ]
    for load in loads:
        load.start()
    for index, ref in enumerate((w1, w2, r1, r2)):
        gbuf[index, place.g] = ref[...]
    enter(place, True)

    def group_copy(part, step, here):
        block = pl.ds(part, 1) if part < 2 else pl.ds(2, 2)
        source = place.g if here else lax.rem(place.g + (N_GROUP - step), N_GROUP)
        ref = gbuf.at[block, source]
        return remote(ref, ref, gsend.at[part, step], grecv.at[part, step], (place.peer(step), place.m))

    for part in range(3):
        for step in range(1, N_GROUP):
            go(group_copy(part, step, True))

    def assemble(index):
        parts = [gbuf[index, group].astype(f32) for group in range(N_GROUP)]
        return jnp.concatenate(parts, axis=1).astype(bf16)

    def slot(w, dist, piece):
        return wbuf.at[w, place.xof(piece), place.zof(-dist), place.core]

    def share(w, dist, piece):
        ref = slot(w, dist, piece)
        go(remote(ref, ref, ssend.at[w, dist % NZ, piece], srecv.at[w, dist % NZ, piece], place.sibling))

    def ring_copy(w, direction, dist, piece, here):
        sign = 1 if direction == 0 else -1
        ref = slot(w, sign * (dist - 1 if here else dist), piece)
        to = place.up if direction == 0 else place.down
        return remote(ref, ref, zsend.at[w, direction, dist, piece], zrecv.at[w, direction, dist, piece], to)

    def forward(w, direction, dist, piece):
        if exists(direction, dist, piece):
            go(ring_copy(w, direction, dist, piece, True))

    def ring_start(w):
        for step in range(1, N_GROUP):
            group_copy(w, step, False).wait_recv()
        whole = assemble(w)
        own[w] = whole
        wbuf[w, place.xh, place.z, place.core] = whole
        mine = slot(w, 0, 0)
        go(remote(mine, mine, xsend.at[w], xrecv.at[w], place.across))

    def ring(w):
        for direction in range(2):
            forward(w, direction, 1, 0)
        share(w, 0, 0)
        yield
        theirs = slot(w, 0, 1)
        remote(theirs, theirs, xsend.at[w], xrecv.at[w], place.across).wait_recv()
        for direction in range(2):
            forward(w, direction, 1, 1)
        share(w, 0, 1)
        yield
        for dist in range(1, 5):
            for piece in range(2):
                for direction in range(2):
                    if exists(direction, dist, piece):
                        ring_copy(w, direction, dist, piece, False).wait_recv()
                        forward(w, direction, dist + 1, piece)
                        share(w, dist if direction == 0 else -dist, piece)
                        yield

    def dense(w):
        for dist in range(NZ):
            for piece in range(2):
                ref = wbuf.at[w, place.xof(piece), place.zof(-dist), 1 - place.core]
                remote(ref, ref, ssend.at[w, dist, piece], srecv.at[w, dist, piece], place.sibling).wait_recv()
        for m in range(N_MEMBER):
            weights[w, ROWS * m : ROWS * (m + 1), :] = wbuf[w, m // 16, (m // 2) % NZ, m % 2]

    def lay(w):
        for m in range(N_MEMBER):
            blocks[w, m // 16, (m // 2) % NZ, m % 2] = grad[ROWS * m : ROWS * (m + 1), :]

    def pair_copy(w, dist, piece):
        src = blocks.at[w, place.xof(piece), place.zof(dist), 1 - place.core]
        dst = sib_in.at[w, dist, piece]
        return remote(src, dst, psend.at[w, dist, piece], precv.at[w, dist, piece], place.sibling)

    def pair(w):
        for dist in (4, 3, 5, 2, 6, 1, 7, 0):
            for piece in range(2):
                go(pair_copy(w, dist, piece))

    def summed(w, dist, piece):
        pair_copy(w, dist, piece).wait_recv()
        return blocks[w, place.xof(piece), place.zof(dist), place.core] + sib_in[w, dist, piece]

    def hop(w, direction, dist, piece):
        to = place.up if direction == 0 else place.down
        if dist == 1:
            src, dst = last_out.at[w, direction, piece], last_in.at[w, direction, piece]
        else:
            src, dst = hop_out.at[w, direction, dist - 2, piece], hop_in.at[w, direction, dist - 2, piece]
        return src, dst, remote(src, dst, rsend.at[w, direction, dist, piece], rrecv.at[w, direction, dist, piece], to)

    def scatter(w):
        for dist in (4, 3, 2, 1):
            for piece in range(2):
                for direction in range(2):
                    if not exists(direction, dist, piece):
                        continue
                    total = summed(w, dist if direction == 0 else NZ - dist, piece)
                    if exists(direction, dist + 1, piece):
                        _, arrived, copy = hop(w, direction, dist + 1, piece)
                        copy.wait_recv()
                        total = total + arrived[...].astype(f32)
                    src, _, copy = hop(w, direction, dist, piece)
                    src[...] = total.astype(src.dtype)
                    go(copy)
                    yield

        def final(piece):
            total = summed(w, 0, piece)
            for direction in range(2):
                _, arrived, copy = hop(w, direction, 1, piece)
                copy.wait_recv()
                total = total + arrived[...]
            return total

        x_out[w] = final(1)
        copy = remote(x_out.at[w], x_in.at[w], ysend.at[w], yrecv.at[w], place.across)
        go(copy)
        yield
        total = final(0)
        copy.wait_recv()
        out = (o1, o2)[w]
        out[...] = own[w].astype(f32) - own[2 + w].astype(f32) * (SCALE * (total + x_in[w]))
        yield

    def rows(index, size=UNIT):
        return pl.ds(index * size, size)

    def fold(values):
        return values.reshape(values.shape[0] // 8, 8, C).sum(axis=0)

    def spread(sums):
        column = sums.sum(axis=0, keepdims=True)
        top = column.astype(bf16)
        rest = column - top.astype(f32)
        middle = rest.astype(bf16)
        low = (rest - middle.astype(f32)).astype(bf16)
        terms = jnp.concatenate([top, middle, low, jnp.zeros((13, C), bf16)], axis=0)
        total = jnp.dot(terms, same_group[...], preferred_element_type=f32)
        return total.sum(axis=0, keepdims=True) * (1.0 / (POINTS * PER_GROUP))

    def sweep(body, start):
        return lax.fori_loop(0, FRAMES, lambda i, carry: body(pl.ds(pl.multiple_of(i * HW, HW), HW), carry), start)

    def padded(i):
        return pl.ds(HW + i * UNIT, UNIT)

    def silu(v):
        return v / (1.0 + jnp.exp(-v))

    first = lax.broadcasted_iota(jnp.int32, (C, C), 0)
    second = lax.broadcasted_iota(jnp.int32, (C, C), 1)
    same_group[...] = (((first * 3277) >> 16) == ((second * 3277) >> 16)).astype(f32).astype(bf16)
    blank = jnp.zeros((HW, C), bf16)
    for ref in (act_one, act_two, err, grad_hid):
        ref[0:HW, :] = blank
        ref[HW + POINTS :, :] = blank
    zero = jnp.zeros((8, C), f32)
    loads[0].wait()
    centre = spread(sweep(lambda at, acc: acc + fold(clip[at, :].astype(f32)), zero))

    def squares(ref, mean):
        def body(at, acc):
            off = ref[at, :].astype(f32) - mean
            return acc + fold(off * off)

        return lax.rsqrt(spread(sweep(body, zero)) + 1e-05)

    ring_start(0)
    ring_one = ring(0)
    next(ring_one)
    inverse = squares(clip, centre)
    next(ring_one)
    units = POINTS // UNIT
    for i in range(units):
        values = (clip[rows(i), :].astype(f32) - centre) * inverse
        act_one[padded(i), :] = silu(values).astype(bf16)
        next(ring_one)
    loads[1].wait()
    bias = jnp.dot(embed[...], proj[...], preferred_element_type=f32)[0:1]
    ring_start(1)
    ring_two = ring(1)
    for i in range(units):
        flip_one[:, rows(i)] = act_one[padded(i), :].T
        next(ring_one, None)
    for _ in ring_one:
        pass
    next(ring_two)
    dense(0)

    def stacked(ref, start, size, taps):
        return jnp.concatenate([ref[pl.ds(start + HW * tap, size), :] for tap in taps], axis=1)

    half = POINTS // 2
    sums = zero
    for part in range(2):
        mixed = jnp.dot(stacked(act_one, part * half, half, (0, 1, 2)), weights[0], preferred_element_type=f32)
        values = SCALE * mixed + bias
        hid[pl.ds(part * half, half), :] = values
        sums = sums + fold(values)
        for _ in range(3):
            next(ring_two)
    centre_two = spread(sums)
    inverse_two = squares(hid, centre_two)
    next(ring_two)
    for i in range(units):
        values = (hid[rows(i), :] - centre_two) * inverse_two
        hid[rows(i), :] = values
        act_two[padded(i), :] = silu(values).astype(bf16)
        next(ring_two, None)
    for i in range(units):
        flip_two[:, rows(i)] = act_two[padded(i), :].T
        next(ring_two, None)
    for _ in ring_two:
        pass
    dense(1)
    loads[2].wait()

    for part in range(2):
        at = pl.ds(part * half, half)
        mixed = jnp.dot(stacked(act_two, part * half, half, (0, 1, 2)), weights[1], preferred_element_type=f32)
        output = clip[at, :].astype(f32) + SCALE * mixed
        err[pl.ds(HW + part * half, half), :] = (output - target[at, :].astype(f32)).astype(bf16)

    def weight_grad(flipped, ref, tap):
        grad[C * tap : C * (tap + 1), :] = jnp.dot(
            flipped[...], ref[pl.ds(HW * (2 - tap), POINTS), :], preferred_element_type=f32
        )

    for tap in range(3):
        weight_grad(flip_two, err, tap)
    lay(1)
    pair(1)

    scatter_two = scatter(1)
    sum_grad, sum_mixed = zero, zero
    for part in range(2):
        at = pl.ds(part * half, half)
        back = jnp.zeros((half, C), f32)
        for tap in range(3):
            back = back + lax.dot_general(
                err[pl.ds(part * half + HW * (2 - tap), half), :],
                weights[1, C * tap : C * (tap + 1), :],
                (((1,), (1,)), ((), ())),
                preferred_element_type=f32,
            )
        values = hid[at, :]
        gate = 1.0 / (1.0 + jnp.exp(-values))
        inner = (SCALE * back) * (gate * (1.0 + values * (1.0 - gate)))
        grad[at, :] = inner
        sum_grad = sum_grad + fold(inner)
        sum_mixed = sum_mixed + fold(inner * values)
        for _ in range(4):
            next(scatter_two)
    mean_grad, mean_mixed = spread(sum_grad), spread(sum_mixed)
    for i in range(units):
        inner = grad[rows(i), :] - mean_grad - hid[rows(i), :] * mean_mixed
        grad_hid[padded(i), :] = (inner * inverse_two).astype(bf16)
        if i % 2:
            next(scatter_two)
    for tap in range(3):
        weight_grad(flip_one, grad_hid, tap)
        next(scatter_two)
    lay(0)
    pair(0)
    for step in range(1, N_GROUP):
        group_copy(2, step, False).wait_recv()
    own[2] = assemble(2)
    own[3] = assemble(3)
    scatter_one = scatter(0)
    for _ in scatter_two:
        next(scatter_one, None)
    for _ in scatter_one:
        pass
    for copy in sends:
        copy.wait_send()


def step(clip, target, time_proj, embed, w1, w2, r1, r2):
    f32, bf16 = jnp.float32, jnp.bfloat16
    dma = pltpu.SemaphoreType.DMA
    vmem = pl.BlockSpec(memory_space=pltpu.VMEM)
    anywhere = pl.BlockSpec(memory_space=pl.ANY)
    block = (ROWS, C)
    wide = (POINTS + 2 * HW, C)
    return pl.pallas_call(
        step_kernel,
        out_shape=(jax.ShapeDtypeStruct(block, f32),) * 2,
        in_specs=[anywhere] * 3 + [vmem] * 5,
        out_specs=(vmem,) * 2,
        scratch_shapes=[
            pltpu.VMEM((POINTS, C), bf16),
            pltpu.VMEM((POINTS, C), bf16),
            pltpu.VMEM(time_proj.shape, bf16),
            pltpu.VMEM((C, C), bf16),
            pltpu.VMEM(wide, bf16),
            pltpu.VMEM(wide, bf16),
            pltpu.VMEM(wide, bf16),
            pltpu.VMEM(wide, bf16),
            pltpu.VMEM((C, POINTS), bf16),
            pltpu.VMEM((C, POINTS), bf16),
            pltpu.VMEM((POINTS, C), f32),
            pltpu.VMEM((2, TAPS, C), bf16),
            pltpu.VMEM((TAPS, C), f32),
            pltpu.VMEM((4, N_GROUP, ROWS, COLS), bf16),
            pltpu.VMEM((2, NX, NZ, NC) + block, bf16),
            pltpu.VMEM((4,) + block, bf16),
            pltpu.VMEM((2, NX, NZ, NC) + block, f32),
            pltpu.VMEM((2, NZ, 2) + block, f32),
            pltpu.VMEM((2, 2, 3, 2) + block, bf16),
            pltpu.VMEM((2, 2, 3, 2) + block, bf16),
            pltpu.VMEM((2, 2, 2) + block, f32),
            pltpu.VMEM((2, 2, 2) + block, f32),
            pltpu.VMEM((2,) + block, f32),
            pltpu.VMEM((2,) + block, f32),
            dma((3,)),
            dma((3, N_GROUP)),
            dma((3, N_GROUP)),
            dma((2, 2, 5, 2)),
            dma((2, 2, 5, 2)),
            dma((2,)),
            dma((2,)),
            dma((2, NZ, 2)),
            dma((2, NZ, 2)),
            dma((2, 2, 5, 2)),
            dma((2, 2, 5, 2)),
            dma((2,)),
            dma((2,)),
            dma((2, NZ, 2)),
            dma((2, NZ, 2)),
        ],
        compiler_params=pltpu.CompilerParams(
            collective_id=0, has_side_effects=True, vmem_limit_bytes=62 << 20
        ),
        name="inner_step",
    )(clip, target, time_proj, embed, w1, w2, r1, r2)


def embed_rows(step_index, ident, subject_table):
    half_width = subject_table.shape[1] // 2
    freqs = jnp.exp(-math.log(10000.0) * jnp.arange(half_width, dtype=jnp.float32) / half_width)
    angles = step_index.astype(jnp.float32) * freqs
    embedding = jnp.concatenate([jnp.cos(angles), jnp.sin(angles)])
    onehot = (jnp.arange(subject_table.shape[0], dtype=jnp.int32) == ident).astype(jnp.float32)
    embedding = embedding + jnp.dot(onehot, subject_table, precision=lax.Precision.HIGHEST)
    activated = jax.nn.silu(embedding).astype(jnp.bfloat16)
    return jnp.broadcast_to(activated[None, :], (16, activated.shape[0]))


def shards(
    clips,
    targets,
    timestep,
    identity,
    conv1_weight,
    conv2_weight,
    rate1,
    rate2,
    time_proj,
    subject_table,
):
    embed = embed_rows(timestep[0], identity[0], subject_table)
    adapted_one, adapted_two = step(
        clips.reshape(POINTS, C),
        targets.reshape(POINTS, C),
        time_proj,
        embed,
        conv1_weight,
        conv2_weight,
        rate1,
        rate2,
    )
    return (adapted_one[None], adapted_two[None])


def solution(mesh):
    return jax.shard_map(
        shards,
        mesh=mesh,
        in_specs=(
            P(("group", "member"), None, None, None),
            P(("group", "member"), None, None, None),
            P(("group", "member")),
            P(("group", "member")),
            P("member", "group"),
            P("member", "group"),
            P("member", "group"),
            P("member", "group"),
            P(),
            P(),
        ),
        out_specs=(P("group", "member", None), P("group", "member", None)),
        check_vma=False,
    )
```

time: 173 us -> 125 us (0.72)
  matrix products: 26.1 us -> 0.24 us
  other arithmetic: 14.2 us -> 0.07 us
  local copies, waits for them, and re-layouts: 11 us -> 4.12 us
    dot_general x7 -> x1, matrix products: 26.1 us -> 0.24 us  [embed_rows(): jnp.dot(onehot, subject_table, precision=lax.Precision.HIGHEST)]
    reduce_sum x11 -> x0, other arithmetic: 8.67 us -> none  [the longest x1 2.82 us: group_norm(): centred = values - centre]
    unnamed x38 -> x4, local copies, waits for them, and re-layouts: 8.28 us -> 3.48 us
    convert_element_type x3 -> x1, other arithmetic: 4.29 us -> 0.02 us  [embed_rows(): activated = jax.nn.silu(embedding).astype(jnp.bfloat16)]
    pallas_call x2 -> x1, Pallas kernels: 119 us -> 118 us  [step(): pl.pallas_call(step_kernel, out_shape=(jax.ShapeDtypeStruct(block, f32),)...]
where the time goes in v2:
time: 125 us
  Pallas kernels  118 us (94%)
  local copies, waits for them, and re-layouts  4.12 us (3%)
  between operations  2.01 us (2%)
    pallas_call x1, Pallas kernels, step(): pl.pallas_call(step_kernel, out_shape=(jax.ShapeDtypeStruct(block, f32),)...  118 us
    unnamed x4, local copies, waits for them, and re-layouts  3.48 us

profile of v2, /device:TPU:8, one launch (start us, length us, event | category | flops | bytes accessed | tf_op | source)
XLA Modules:
  0.0 124.6 jit_solution(7773277554520362328)
XLA Ops:
  0.6 0.0 copy-start
  2.0 0.0 copy-done
  2.0 0.2 convolution_reduce_fusion
  2.2 0.1 fusion
  2.3 0.6 broadcast_in_dim.12.embed
  3.0 118.2 %inner_step.1 = (f32[60,640]{1,0:T(8,128)}, f32[60,640]{1,0:T(8,128)}) custom-call(bf16[896,640]{1,0:T(8,128)(2,1)} %bitcast.11, bf16[896,640]{1,0:T(8,128)(2,1)} %bitcast.12, bf16[1280,640]{1,0:T(8,128)(2,1)} %proj_hbm.1, bf16[16,1280]{1,0:T(8,128)(2,1)} %broadcast_in_dim.12.embed, bf16[60,80]{1,0:T(8,128)(2,1)} %w1.1, bf16[60,80]{1,0:T(8,128)(2,1)} %w2.1, ...), custom_call_target="tpu_custom_call" | custom-call | tf_op jit(solution)/shard_map/inner_step/pallas_call | solution.py:382
  121.1 1.7 %copy.12 = f32[1,60,640]{2,0,1:T(1,128)} copy(f32[1,60,640]{2,1,0:T(8,128)} %bitcast.14) | data formatting | bytes 307200
  122.9 1.7 %copy.13 = f32[1,60,640]{2,0,1:T(1,128)} copy(f32[1,60,640]{2,1,0:T(8,128)} %bitcast.13) | data formatting | bytes 307200
  (1 shorter events, 0.0 us)
Async XLA Ops:
  0.6 1.4 %copy-start = (f32[64,1280]{1,0:T(8,128)S(1)}, f32[64,1280]{1,0:T(8,128)}, u32[]{:S(2)}) copy-start(f32[64,1280]{1,0:T(8,128)} %param.19) | copy-start | bytes 983044

commit v3 on v2

--- a/solution.py
+++ b/solution.py
@@ -32,6 +32,10 @@
         self.down = self.at(self.xh, self.zof(-1), self.core)
         self.across = self.at(1 - self.xh, self.z, self.core)
         self.sibling = self.at(self.xh, self.z, 1 - self.core)
+        self.x_lo = lax.rem(self.g, 2)
+        self.y_lo = lax.rem(lax.div(self.g, 2), 2)
+        self.beside_x = (self.g + 1 - 2 * self.x_lo, self.m)
+        self.beside_y = (self.g + 2 - 4 * self.y_lo, self.m)
 
     def at(self, xh, z, core):
         return (self.g, (xh * NZ + z) * 2 + core)
@@ -70,7 +74,7 @@
     clip_hbm, target_hbm, proj_hbm, embed, w1, w2, r1, r2, o1, o2,
     clip, target, proj, same_group, act_one, act_two, err, grad_hid, flip_one, flip_two, hid, weights, grad,
     gbuf, wbuf, own, blocks, sib_in, hop_out, hop_in, last_out, last_in, x_out, x_in,
-    load_sem, gsend, grecv, zsend, zrecv, xsend, xrecv, ssend, srecv,
+    load_sem, gsend, grecv, zsend, zrecv, xsend, xrecv, ssend, srecv, bsend, brecv,
     rsend, rrecv, ysend, yrecv, psend, precv,
 ):
     f32, bf16 = jnp.float32, jnp.bfloat16
@@ -97,24 +101,36 @@
         ref = gbuf.at[block, source]
         return remote(ref, ref, gsend.at[part, step], grecv.at[part, step], (place.peer(step), place.m))
 
-    for part in range(3):
+    def group_send(part):
         for step in range(1, N_GROUP):
             go(group_copy(part, step, True))
 
+    group_send(0)
+    group_send(1)
+
     def assemble(index):
         parts = [gbuf[index, group].astype(f32) for group in range(N_GROUP)]
-        return jnp.concatenate(parts, axis=1).astype(bf16)
-
-    def slot(w, dist, piece):
-        return wbuf.at[w, place.xof(piece), place.zof(-dist), place.core]
-
-    def share(w, dist, piece):
-        ref = slot(w, dist, piece)
-        go(remote(ref, ref, ssend.at[w, dist % NZ, piece], srecv.at[w, dist % NZ, piece], place.sibling))
+        return jnp.concatenate(parts, axis=1)
+
+    tile_slot = (2 * place.x_lo, 2 - 2 * place.x_lo, 1 + 2 * place.y_lo, 3 - 2 * place.y_lo)
+
+    def slot(w, dist, piece, first, count, core=None):
+        core = place.core if core is None else core
+        return wbuf.at[w, place.xof(piece), place.zof(-dist), core, pl.ds(first, count)]
+
+    def share_copy(w, dist, piece, high, count, here):
+        ref = slot(w, dist, piece, 2 * high, count, place.core if here else 1 - place.core)
+        at = (w, high, dist % NZ, piece)
+        return remote(ref, ref, ssend.at[at], srecv.at[at], place.sibling)
+
+    def side_copy(w, side, dist, piece):
+        src, dst = slot(w, dist, piece, side, 1), slot(w, dist, piece, side + 2, 1)
+        at = (w, side, dist % NZ, piece)
+        return remote(src, dst, bsend.at[at], brecv.at[at], (place.beside_x, place.beside_y)[side])
 
     def ring_copy(w, direction, dist, piece, here):
         sign = 1 if direction == 0 else -1
-        ref = slot(w, sign * (dist - 1 if here else dist), piece)
+        ref = slot(w, sign * (dist - 1 if here else dist), piece, 0, 2)
         to = place.up if direction == 0 else place.down
         return remote(ref, ref, zsend.at[w, direction, dist, piece], zrecv.at[w, direction, dist, piece], to)
 
@@ -122,42 +138,64 @@
         if exists(direction, dist, piece):
             go(ring_copy(w, direction, dist, piece, True))
 
+    def hand_on(w, dist, piece):
+        for side in range(2):
+            go(side_copy(w, side, dist, piece))
+        go(share_copy(w, dist, piece, 0, 2, True))
+
+    def across_copy(w, piece):
+        ref = slot(w, 0, piece, 0, 2)
+        return remote(ref, ref, xsend.at[w], xrecv.at[w], place.across)
+
     def ring_start(w):
         for step in range(1, N_GROUP):
             group_copy(w, step, False).wait_recv()
-        whole = assemble(w)
-        own[w] = whole
-        wbuf[w, place.xh, place.z, place.core] = whole
-        mine = slot(w, 0, 0)
-        go(remote(mine, mine, xsend.at[w], xrecv.at[w], place.across))
-
-    def ring(w):
+        whole = jnp.concatenate([assemble(w), jnp.zeros((4, C), f32)], axis=0).astype(bf16)
+        own[w] = whole[0:ROWS]
+        for tile in range(4):
+            wbuf[w, place.xh, place.z, place.core, tile_slot[tile]] = whole[16 * tile : 16 * (tile + 1)]
+        go(across_copy(w, 0))
         for direction in range(2):
             forward(w, direction, 1, 0)
-        share(w, 0, 0)
-        yield
-        theirs = slot(w, 0, 1)
-        remote(theirs, theirs, xsend.at[w], xrecv.at[w], place.across).wait_recv()
+        go(share_copy(w, 0, 0, 0, 4, True))
+
+    def ring_across(w):
+        across_copy(w, 1).wait_recv()
         for direction in range(2):
             forward(w, direction, 1, 1)
-        share(w, 0, 1)
-        yield
-        for dist in range(1, 5):
-            for piece in range(2):
-                for direction in range(2):
-                    if exists(direction, dist, piece):
-                        ring_copy(w, direction, dist, piece, False).wait_recv()
-                        forward(w, direction, dist + 1, piece)
-                        share(w, dist if direction == 0 else -dist, piece)
-                        yield
+        hand_on(w, 0, 1)
+
+    def ring_step(w, dist):
+        for piece in range(2):
+            for direction in range(2):
+                if exists(direction, dist, piece):
+                    ring_copy(w, direction, dist, piece, False).wait_recv()
+                    forward(w, direction, dist + 1, piece)
+                    hand_on(w, dist if direction == 0 else -dist, piece)
+
+    def ring_sides(w, dist):
+        for piece in range(2):
+            for direction in range(2):
+                far = dist if direction == 0 else -dist
+                if not exists(direction, dist, piece) or dist == 0 and (direction == 1 or piece == 0):
+                    continue
+                for side in range(2):
+                    side_copy(w, side, far, piece).wait_recv()
+                go(share_copy(w, far, piece, 1, 2, True))
 
     def dense(w):
         for dist in range(NZ):
             for piece in range(2):
-                ref = wbuf.at[w, place.xof(piece), place.zof(-dist), 1 - place.core]
-                remote(ref, ref, ssend.at[w, dist, piece], srecv.at[w, dist, piece], place.sibling).wait_recv()
+                if (dist, piece) == (0, 0):
+                    share_copy(w, dist, piece, 0, 4, False).wait_recv()
+                else:
+                    share_copy(w, dist, piece, 0, 2, False).wait_recv()
+                    share_copy(w, dist, piece, 1, 2, False).wait_recv()
         for m in range(N_MEMBER):
-            weights[w, ROWS * m : ROWS * (m + 1), :] = wbuf[w, m // 16, (m // 2) % NZ, m % 2]
+            for tile in range(4):
+                start, size = ROWS * m + 16 * tile, min(16, ROWS - 16 * tile)
+                block = wbuf[w, m // 16, (m // 2) % NZ, m % 2, tile_slot[tile]]
+                weights[w, start : start + size, :] = block[0:size]
 
     def lay(w):
         for m in range(N_MEMBER):
@@ -262,26 +300,49 @@
 
         return lax.rsqrt(spread(sweep(body, zero)) + 1e-05)
 
-    ring_start(0)
-    ring_one = ring(0)
-    next(ring_one)
     inverse = squares(clip, centre)
-    next(ring_one)
     units = POINTS // UNIT
-    for i in range(units):
+
+    def act_unit(i):
         values = (clip[rows(i), :].astype(f32) - centre) * inverse
         act_one[padded(i), :] = silu(values).astype(bf16)
-        next(ring_one)
+
+    def flip_unit(flipped, ref, i):
+        flipped[:, rows(i)] = ref[padded(i), :].T
+
+    ring_start(0)
+    act_unit(0)
+    act_unit(1)
+    act_unit(2)
+    ring_across(0)
+    ring_start(1)
+    act_unit(3)
+    ring_step(0, 1)
+    act_unit(4)
+    ring_across(1)
+    ring_sides(0, 0)
+    act_unit(5)
+    ring_step(0, 2)
+    ring_step(1, 1)
+    act_unit(6)
+    ring_sides(0, 1)
     loads[1].wait()
     bias = jnp.dot(embed[...], proj[...], preferred_element_type=f32)[0:1]
-    ring_start(1)
-    ring_two = ring(1)
-    for i in range(units):
-        flip_one[:, rows(i)] = act_one[padded(i), :].T
-        next(ring_one, None)
-    for _ in ring_one:
-        pass
-    next(ring_two)
+    ring_step(0, 3)
+    ring_step(1, 2)
+    ring_sides(1, 0)
+    for i in range(3):
+        flip_unit(flip_one, act_one, i)
+    ring_sides(0, 2)
+    ring_step(0, 4)
+    ring_step(1, 3)
+    ring_sides(1, 1)
+    for i in range(3, units):
+        flip_unit(flip_one, act_one, i)
+    ring_sides(0, 3)
+    ring_sides(0, 4)
+    ring_step(1, 4)
+    ring_sides(1, 2)
     dense(0)
 
     def stacked(ref, start, size, taps):
@@ -294,21 +355,16 @@
         values = SCALE * mixed + bias
         hid[pl.ds(part * half, half), :] = values
         sums = sums + fold(values)
-        for _ in range(3):
-            next(ring_two)
+        ring_sides(1, 3 + part)
+    group_send(2)
     centre_two = spread(sums)
     inverse_two = squares(hid, centre_two)
-    next(ring_two)
     for i in range(units):
         values = (hid[rows(i), :] - centre_two) * inverse_two
         hid[rows(i), :] = values
         act_two[padded(i), :] = silu(values).astype(bf16)
-        next(ring_two, None)
     for i in range(units):
-        flip_two[:, rows(i)] = act_two[padded(i), :].T
-        next(ring_two, None)
-    for _ in ring_two:
-        pass
+        flip_unit(flip_two, act_two, i)
     dense(1)
     loads[2].wait()
 
@@ -361,8 +417,8 @@
     pair(0)
     for step in range(1, N_GROUP):
         group_copy(2, step, False).wait_recv()
-    own[2] = assemble(2)
-    own[3] = assemble(3)
+    own[2] = assemble(2).astype(bf16)
+    own[3] = assemble(3).astype(bf16)
     scatter_one = scatter(0)
     for _ in scatter_two:
         next(scatter_one, None)
@@ -399,7 +455,7 @@
             pltpu.VMEM((2, TAPS, C), bf16),
             pltpu.VMEM((TAPS, C), f32),
             pltpu.VMEM((4, N_GROUP, ROWS, COLS), bf16),
-            pltpu.VMEM((2, NX, NZ, NC) + block, bf16),
+            pltpu.VMEM((2, NX, NZ, NC, 4, 16, C), bf16),
             pltpu.VMEM((4,) + block, bf16),
             pltpu.VMEM((2, NX, NZ, NC) + block, f32),
             pltpu.VMEM((2, NZ, 2) + block, f32),
@@ -416,8 +472,10 @@
             dma((2, 2, 5, 2)),
             dma((2,)),
             dma((2,)),
-            dma((2, NZ, 2)),
-            dma((2, NZ, 2)),
+            dma((2, 2, NZ, 2)),
+            dma((2, 2, NZ, 2)),
+            dma((2, 2, NZ, 2)),
+            dma((2, 2, NZ, 2)),
             dma((2, 2, 5, 2)),
             dma((2, 2, 5, 2)),
             dma((2,)),

time: 125 us -> 113 us (0.904)
  Pallas kernels: 118 us -> 106 us
    pallas_call x1, Pallas kernels: 118 us -> 106 us  [step(): pl.pallas_call(step_kernel, out_shape=(jax.ShapeDtypeStruct(block, f32),)...]
where the time goes in v3:
time: 113 us; the launch traced here: 112 us
  Pallas kernels  106 us (94%)
  local copies, waits for them, and re-layouts  4.12 us (4%)
  between operations  2.01 us (2%)
    pallas_call x1, Pallas kernels, step(): pl.pallas_call(step_kernel, out_shape=(jax.ShapeDtypeStruct(block, f32),)...  106 us
    unnamed x4, local copies, waits for them, and re-layouts  3.48 us

profile of v3, /device:TPU:8, one launch (start us, length us, event | category | flops | bytes accessed | tf_op | source)
XLA Modules:
  0.0 112.3 jit_solution(10672770840488414466)
XLA Ops:
  0.6 0.0 copy-start
  2.0 0.0 copy-done
  2.0 0.2 convolution_reduce_fusion
  2.2 0.1 fusion
  2.3 0.6 broadcast_in_dim.12.embed
  3.0 105.9 %inner_step.1 = (f32[60,640]{1,0:T(8,128)}, f32[60,640]{1,0:T(8,128)}) custom-call(bf16[896,640]{1,0:T(8,128)(2,1)} %bitcast.11, bf16[896,640]{1,0:T(8,128)(2,1)} %bitcast.12, bf16[1280,640]{1,0:T(8,128)(2,1)} %proj_hbm.1, bf16[16,1280]{1,0:T(8,128)(2,1)} %broadcast_in_dim.12.embed, bf16[60,80]{1,0:T(8,128)(2,1)} %w1.1, bf16[60,80]{1,0:T(8,128)(2,1)} %w2.1, ...), custom_call_target="tpu_custom_call" | custom-call | tf_op jit(solution)/shard_map/inner_step/pallas_call | solution.py:438
  108.8 1.7 %copy.12 = f32[1,60,640]{2,0,1:T(1,128)} copy(f32[1,60,640]{2,1,0:T(8,128)} %bitcast.14) | data formatting | bytes 307200
  110.6 1.7 %copy.13 = f32[1,60,640]{2,0,1:T(1,128)} copy(f32[1,60,640]{2,1,0:T(8,128)} %bitcast.13) | data formatting | bytes 307200
  (1 shorter events, 0.0 us)
Async XLA Ops:
  0.6 1.4 %copy-start = (f32[64,1280]{1,0:T(8,128)S(1)}, f32[64,1280]{1,0:T(8,128)}, u32[]{:S(2)}) copy-start(f32[64,1280]{1,0:T(8,128)} %param.19) | copy-start | bytes 983044

commit v4 on v3

--- a/solution.py
+++ b/solution.py
@@ -18,6 +18,7 @@
 PER_GROUP = C // GN_GROUPS
 SCALE = 1.0 / math.sqrt(TAPS)
 UNIT = 128
+PART = 32
 
 
 class Place:
@@ -71,11 +72,11 @@
 
 
 def step_kernel(
-    clip_hbm, target_hbm, proj_hbm, embed, w1, w2, r1, r2, o1, o2,
+    clip_hbm, target_hbm, proj_hbm, embed, w1, w2, r1, r2, total_out, own,
     clip, target, proj, same_group, act_one, act_two, err, grad_hid, flip_one, flip_two, hid, weights, grad,
-    gbuf, wbuf, own, blocks, sib_in, hop_out, hop_in, last_out, last_in, x_out, x_in,
+    gbuf, wbuf, blocks, sib_in, cross_out, cross_in, hop_out, hop_in, last_out, last_in, x_out, x_out_own, x_in,
     load_sem, gsend, grecv, zsend, zrecv, xsend, xrecv, ssend, srecv, bsend, brecv,
-    rsend, rrecv, ysend, yrecv, psend, precv,
+    rsend, rrecv, ysend, yrecv, psend, precv, csend, crecv,
 ):
     f32, bf16 = jnp.float32, jnp.bfloat16
     place = Place()
@@ -171,6 +172,8 @@
                 if exists(direction, dist, piece):
                     ring_copy(w, direction, dist, piece, False).wait_recv()
                     forward(w, direction, dist + 1, piece)
+            for direction in range(2):
+                if exists(direction, dist, piece):
                     hand_on(w, dist if direction == 0 else -dist, piece)
 
     def ring_sides(w, dist):
@@ -199,7 +202,9 @@
 
     def lay(w):
         for m in range(N_MEMBER):
-            blocks[w, m // 16, (m // 2) % NZ, m % 2] = grad[ROWS * m : ROWS * (m + 1), :]
+            for part in range(2):
+                start = ROWS * m + PART * part
+                blocks[w, m // 16, (m // 2) % NZ, m % 2, part] = grad[start : start + PART, :]
 
     def pair_copy(w, dist, piece):
         src = blocks.at[w, place.xof(piece), place.zof(dist), 1 - place.core]
@@ -208,54 +213,136 @@
 
     def pair(w):
         for dist in (4, 3, 5, 2, 6, 1, 7, 0):
-            for piece in range(2):
+            for piece in (1, 0):
                 go(pair_copy(w, dist, piece))
 
-    def summed(w, dist, piece):
-        pair_copy(w, dist, piece).wait_recv()
-        return blocks[w, place.xof(piece), place.zof(dist), place.core] + sib_in[w, dist, piece]
-
-    def hop(w, direction, dist, piece):
+    paired = set()
+
+    def summed(w, dist, piece, part):
+        if (w, dist, piece) not in paired:
+            paired.add((w, dist, piece))
+            pair_copy(w, dist, piece).wait_recv()
+        return blocks[w, place.xof(piece), place.zof(dist), place.core, part] + sib_in[w, dist, piece, part]
+
+    def cross_copy(w, dist):
+        return remote(cross_out.at[w, dist], cross_in.at[w, dist], csend.at[w, dist], crecv.at[w, dist], place.across)
+
+    def cross(w, *dists):
+        for dist in dists:
+            cross_out[w, dist] = summed(w, dist, 1, 0).astype(bf16)
+            go(cross_copy(w, dist))
+
+    def crossed(w, dist):
+        cross_copy(w, dist).wait_recv()
+        return summed(w, dist, 0, 0) + cross_in[w, dist].astype(f32)
+
+    def hop(w, part, direction, dist):
         to = place.up if direction == 0 else place.down
         if dist == 1:
-            src, dst = last_out.at[w, direction, piece], last_in.at[w, direction, piece]
+            src, dst = last_out.at[w, direction], last_in.at[w, direction]
         else:
-            src, dst = hop_out.at[w, direction, dist - 2, piece], hop_in.at[w, direction, dist - 2, piece]
-        return src, dst, remote(src, dst, rsend.at[w, direction, dist, piece], rrecv.at[w, direction, dist, piece], to)
+            src, dst = hop_out.at[w, direction, dist - 2], hop_in.at[w, direction, dist - 2]
+        if part == 1:
+            take = pl.ds(direction, 1) if dist == 4 else pl.ds(0, 2)
+            src, dst = src.at[take], dst.at[take]
+        else:
+            take = pl.ds(16 * direction, 16) if dist == 4 else pl.ds(0, PART)
+            src, dst = src.at[2, take], dst.at[2, take]
+        return src, dst, remote(src, dst, rsend.at[w, part, direction, dist], rrecv.at[w, part, direction, dist], to)
+
+    def far(direction, dist):
+        return dist if direction == 0 else NZ - dist
+
+    def ring_z(w, dist):
+        for direction in range(2):
+            arrived = None
+            if dist < 4:
+                _, arrived, copy = hop(w, 1, direction, dist + 1)
+                copy.wait_recv()
+            src, _, copy = hop(w, 1, direction, dist)
+            for piece in (direction,) if dist == 4 else (0, 1):
+                total = summed(w, far(direction, dist), piece, 1)
+                if dist < 3:
+                    total = total + arrived[piece].astype(f32)
+                elif dist == 3 and piece == direction:
+                    total = total + arrived[0].astype(f32)
+                src[0 if dist == 4 else piece] = total.astype(src.dtype)
+            go(copy)
+
+    def ring_x(w, dist):
+        own_sum = crossed(w, 4) if dist == 4 else None
+        for direction in range(2):
+            src, _, copy = hop(w, 0, direction, dist)
+            if dist == 4:
+                src[...] = own_sum[16 * direction : 16 * (direction + 1)].astype(src.dtype)
+            else:
+                _, arrived, before = hop(w, 0, direction, dist + 1)
+                total = crossed(w, far(direction, dist))
+                before.wait_recv()
+                if dist == 3:
+                    low, high = total[:16], total[16:]
+                    if direction == 0:
+                        low = low + arrived[...].astype(f32)
+                    else:
+                        high = high + arrived[...].astype(f32)
+                    src[0:16] = low.astype(src.dtype)
+                    src[16:PART] = high.astype(src.dtype)
+                else:
+                    src[...] = (total + arrived[...].astype(f32)).astype(src.dtype)
+            go(copy)
+
+    def swap_copy(w):
+        return remote(x_out.at[w], x_in.at[w], ysend.at[w], yrecv.at[w], place.across)
+
+    def finish_z(w):
+        parts = [summed(w, 0, piece, 1) for piece in range(2)]
+        for direction in range(2):
+            _, arrived, copy = hop(w, 1, direction, 1)
+            copy.wait_recv()
+            parts = [parts[piece] + arrived[piece] for piece in range(2)]
+        x_out[w] = parts[1]
+        go(swap_copy(w))
+        x_out_own[w] = parts[0]
+
+    def finish_x(w):
+        total = crossed(w, 0)
+        for direction in range(2):
+            _, arrived, copy = hop(w, 0, direction, 1)
+            copy.wait_recv()
+            total = total + arrived[...]
+        total_out[w, 0:PART] = SCALE * total
+
+    def finish(w):
+        swap_copy(w).wait_recv()
+        total_out[w, PART:ROWS] = (SCALE * (x_out_own[w] + x_in[w]))[0 : ROWS - PART]
 
     def scatter(w):
-        for dist in (4, 3, 2, 1):
-            for piece in range(2):
-                for direction in range(2):
-                    if not exists(direction, dist, piece):
-                        continue
-                    total = summed(w, dist if direction == 0 else NZ - dist, piece)
-                    if exists(direction, dist + 1, piece):
-                        _, arrived, copy = hop(w, direction, dist + 1, piece)
-                        copy.wait_recv()
-                        total = total + arrived[...].astype(f32)
-                    src, _, copy = hop(w, direction, dist, piece)
-                    src[...] = total.astype(src.dtype)
-                    go(copy)
-                    yield
-
-        def final(piece):
-            total = summed(w, 0, piece)
-            for direction in range(2):
-                _, arrived, copy = hop(w, direction, 1, piece)
-                copy.wait_recv()
-                total = total + arrived[...]
-            return total
-
-        x_out[w] = final(1)
-        copy = remote(x_out.at[w], x_in.at[w], ysend.at[w], yrecv.at[w], place.across)
-        go(copy)
-        yield
-        total = final(0)
-        copy.wait_recv()
-        out = (o1, o2)[w]
-        out[...] = own[w].astype(f32) - own[2 + w].astype(f32) * (SCALE * (total + x_in[w]))
-        yield
+        cross(w, 4)
+        ring_z(w, 4)
+        yield
+        cross(w, 3, 5)
+        yield
+        ring_z(w, 3)
+        cross(w, 2, 6)
+        yield
+        ring_x(w, 4)
+        yield
+        ring_z(w, 2)
+        cross(w, 1, 7, 0)
+        yield
+        ring_x(w, 3)
+        yield
+        ring_z(w, 1)
+        yield
+        ring_x(w, 2)
+        yield
+        finish_z(w)
+        yield
+        ring_x(w, 1)
+        yield
+        finish_x(w)
+        yield
+        finish(w)
 
     def rows(index, size=UNIT):
         return pl.ds(index * size, size)
@@ -290,6 +377,7 @@
         ref[0:HW, :] = blank
         ref[HW + POINTS :, :] = blank
     zero = jnp.zeros((8, C), f32)
+    grad[TAPS:, :] = zero
     loads[0].wait()
     centre = spread(sweep(lambda at, acc: acc + fold(clip[at, :].astype(f32)), zero))
 
@@ -402,14 +490,12 @@
         grad[at, :] = inner
         sum_grad = sum_grad + fold(inner)
         sum_mixed = sum_mixed + fold(inner * values)
-        for _ in range(4):
-            next(scatter_two)
+        next(scatter_two)
+        next(scatter_two)
     mean_grad, mean_mixed = spread(sum_grad), spread(sum_mixed)
     for i in range(units):
         inner = grad[rows(i), :] - mean_grad - hid[rows(i), :] * mean_mixed
         grad_hid[padded(i), :] = (inner * inverse_two).astype(bf16)
-        if i % 2:
-            next(scatter_two)
     for tap in range(3):
         weight_grad(flip_one, grad_hid, tap)
         next(scatter_two)
@@ -420,6 +506,7 @@
     own[2] = assemble(2).astype(bf16)
     own[3] = assemble(3).astype(bf16)
     scatter_one = scatter(0)
+    next(scatter_one)
     for _ in scatter_two:
         next(scatter_one, None)
     for _ in scatter_one:
@@ -433,11 +520,11 @@
     dma = pltpu.SemaphoreType.DMA
     vmem = pl.BlockSpec(memory_space=pltpu.VMEM)
     anywhere = pl.BlockSpec(memory_space=pl.ANY)
-    block = (ROWS, C)
+    part = (PART, C)
     wide = (POINTS + 2 * HW, C)
     return pl.pallas_call(
         step_kernel,
-        out_shape=(jax.ShapeDtypeStruct(block, f32),) * 2,
+        out_shape=(jax.ShapeDtypeStruct((2, ROWS, C), f32), jax.ShapeDtypeStruct((4, ROWS, C), bf16)),
         in_specs=[anywhere] * 3 + [vmem] * 5,
         out_specs=(vmem,) * 2,
         scratch_shapes=[
@@ -453,18 +540,20 @@
             pltpu.VMEM((C, POINTS), bf16),
             pltpu.VMEM((POINTS, C), f32),
             pltpu.VMEM((2, TAPS, C), bf16),
-            pltpu.VMEM((TAPS, C), f32),
+            pltpu.VMEM((TAPS + 8, C), f32),
             pltpu.VMEM((4, N_GROUP, ROWS, COLS), bf16),
             pltpu.VMEM((2, NX, NZ, NC, 4, 16, C), bf16),
-            pltpu.VMEM((4,) + block, bf16),
-            pltpu.VMEM((2, NX, NZ, NC) + block, f32),
-            pltpu.VMEM((2, NZ, 2) + block, f32),
-            pltpu.VMEM((2, 2, 3, 2) + block, bf16),
-            pltpu.VMEM((2, 2, 3, 2) + block, bf16),
-            pltpu.VMEM((2, 2, 2) + block, f32),
-            pltpu.VMEM((2, 2, 2) + block, f32),
-            pltpu.VMEM((2,) + block, f32),
-            pltpu.VMEM((2,) + block, f32),
+            pltpu.VMEM((2, NX, NZ, NC, 2) + part, f32),
+            pltpu.VMEM((2, NZ, 2, 2) + part, f32),
+            pltpu.VMEM((2, NZ) + part, bf16),
+            pltpu.VMEM((2, NZ) + part, bf16),
+            pltpu.VMEM((2, 2, 3, 3) + part, bf16),
+            pltpu.VMEM((2, 2, 3, 3) + part, bf16),
+            pltpu.VMEM((2, 2, 3) + part, f32),
+            pltpu.VMEM((2, 2, 3) + part, f32),
+            pltpu.VMEM((2,) + part, f32),
+            pltpu.VMEM((2,) + part, f32),
+            pltpu.VMEM((2,) + part, f32),
             dma((3,)),
             dma((3, N_GROUP)),
             dma((3, N_GROUP)),
@@ -476,12 +565,14 @@
             dma((2, 2, NZ, 2)),
             dma((2, 2, NZ, 2)),
             dma((2, 2, NZ, 2)),
-            dma((2, 2, 5, 2)),
-            dma((2, 2, 5, 2)),
+            dma((2, 2, 2, 5)),
+            dma((2, 2, 2, 5)),
             dma((2,)),
             dma((2,)),
             dma((2, NZ, 2)),
             dma((2, NZ, 2)),
+            dma((2, NZ)),
+            dma((2, NZ)),
         ],
         compiler_params=pltpu.CompilerParams(
             collective_id=0, has_side_effects=True, vmem_limit_bytes=62 << 20
@@ -514,7 +605,7 @@
     subject_table,
 ):
     embed = embed_rows(timestep[0], identity[0], subject_table)
-    adapted_one, adapted_two = step(
+    total, own = step(
         clips.reshape(POINTS, C),
         targets.reshape(POINTS, C),
         time_proj,
@@ -524,7 +615,8 @@
         rate1,
         rate2,
     )
-    return (adapted_one[None], adapted_two[None])
+    own = own.astype(jnp.float32)
+    return tuple((own[w] - own[2 + w] * total[w])[None] for w in range(2))
 
 
 def solution(mesh):

time: 113 us -> 100 us (0.88)
  Pallas kernels: 106 us -> 94.2 us
  local copies, waits for them, and re-layouts: 4.12 us -> 2.29 us
    pallas_call x1, Pallas kernels: 106 us -> 94.2 us  [step(): pl.pallas_call(step_kernel, out_shape=(jax.ShapeDtypeStruct((2, ROWS, C),...]
    unnamed x4 -> x6, local copies, waits for them, and re-layouts: 3.48 us -> 1.66 us
where the time goes in v4:
time: 100 us
  Pallas kernels  94.2 us (94%)
  local copies, waits for them, and re-layouts  2.29 us (2%)
  between operations  2.04 us (2%)
  other arithmetic  1.18 us (1%)
    pallas_call x1, Pallas kernels, step(): pl.pallas_call(step_kernel, out_shape=(jax.ShapeDtypeStruct((2, ROWS, C),...  94.2 us

profile of v4, /device:TPU:8, one launch (start us, length us, event | category | flops | bytes accessed | tf_op | source)
XLA Modules:
  0.0 100.0 jit_solution(9621739609829623080)
XLA Ops:
  0.6 0.0 copy-start
  2.0 0.0 copy-done
  2.0 0.2 convolution_reduce_fusion
  2.2 0.1 fusion.2
  2.3 0.6 broadcast_in_dim.2.embed
  3.0 94.2 %inner_step.1 = (f32[2,60,640]{2,1,0:T(8,128)}, bf16[4,60,640]{2,1,0:T(8,128)(2,1)}) custom-call(bf16[896,640]{1,0:T(8,128)(2,1)} %bitcast.9, bf16[896,640]{1,0:T(8,128)(2,1)} %bitcast.10, bf16[1280,640]{1,0:T(8,128)(2,1)} %proj_hbm.1, bf16[16,1280]{1,0:T(8,128)(2,1)} %broadcast_in_dim.2.embed, bf16[60,80]{1,0:T(8,128)(2,1)} %w1.1, bf16[60,80]{1,0:T(8,128)(2,1)} %w2.1, ...), custom_call_target="tpu_custom_call" | custom-call | tf_op jit(solution)/shard_map/inner_step/pallas_call | solution.py:525
  97.2 0.0 copy-start.1
  97.2 1.1 %convert_element_type.16 = f32[4,60,640]{2,1,0:T(8,128)S(1)} convert(bf16[4,60,640]{2,1,0:T(8,128)(2,1)} %get-tuple-element.4) | non-fusion elementwise | flops 153600 | bytes 921600 | tf_op jit(solution)/shard_map/convert_element_type | solution.py:618
  98.3 0.0 copy-done.1
  98.3 0.1 fusion
  98.3 0.8 copy.13
  99.2 0.8 copy.12
  (1 shorter events, 0.0 us)
Async XLA Ops:
  0.6 1.4 %copy-start = (f32[64,1280]{1,0:T(8,128)S(1)}, f32[64,1280]{1,0:T(8,128)}, u32[]{:S(2)}) copy-start(f32[64,1280]{1,0:T(8,128)} %param.19) | copy-start | bytes 983044
  97.2 1.1 %copy-start.1 = (f32[2,60,640]{2,1,0:T(8,128)S(1)}, f32[2,60,640]{2,1,0:T(8,128)}, u32[]{:S(2)}) copy-start(f32[2,60,640]{2,1,0:T(8,128)} %get-tuple-element.5) | copy-start | bytes 921604

commit v5 on v4

v5 whole, which is shorter than its diff:
```python
import functools
import math

import jax
import jax.numpy as jnp
import numpy as np
from jax import lax
from jax.experimental import pallas as pl
from jax.experimental.pallas import tpu as pltpu
from jax.sharding import PartitionSpec as P

GN_GROUPS = 32
MESH = pl.DeviceIdType.MESH
N_GROUP, N_MEMBER, NZ, NC, NX = 8, 32, 8, 2, 2
ROWS, COLS, C = 60, 80, 640
TAPS = 3 * C
FRAMES, HW = 14, 64
POINTS = FRAMES * HW
PER_GROUP = C // GN_GROUPS
SCALE = 1.0 / math.sqrt(TAPS)
UNIT = 128
PART = 32


class Place:
    def __init__(self):
        self.g = lax.axis_index("group")
        self.m = lax.axis_index("member")
        self.core = lax.rem(self.m, 2)
        self.q = lax.div(self.m, 2)
        self.z = lax.rem(self.q, NZ)
        self.xh = lax.div(self.q, NZ)
        self.up = self.at(self.xh, self.zof(1), self.core)
        self.down = self.at(self.xh, self.zof(-1), self.core)
        self.across = self.at(1 - self.xh, self.z, self.core)
        self.sibling = self.at(self.xh, self.z, 1 - self.core)
        self.x_lo = lax.rem(self.g, 2)
        self.y_lo = lax.rem(lax.div(self.g, 2), 2)
        self.beside_x = (self.g + 1 - 2 * self.x_lo, self.m)
        self.beside_y = (self.g + 2 - 4 * self.y_lo, self.m)
        self.opposite = self.across[1]
        self.twin = self.sibling[1]

    def at(self, xh, z, core):
        return (self.g, (xh * NZ + z) * 2 + core)

    def zof(self, step):
        return lax.rem(self.z + (step + NZ), NZ)

    def peer(self, step):
        return lax.rem(self.g + step, N_GROUP)

    def xof(self, piece):
        return self.xh if piece == 0 else 1 - self.xh


def remote(src, dst, send, recv, device):
    return pltpu.make_async_remote_copy(
        src_ref=src, dst_ref=dst, send_sem=send, recv_sem=recv, device_id=device, device_id_type=MESH
    )


def partners(place):
    plane = [((place.peer(step), place.m)) for step in range(1, N_GROUP)]
    beyond = [((place.peer(step), place.opposite)) for step in range(N_GROUP)]
    sides = [(place.beside_x[0], place.twin), (place.beside_y[0], place.twin)]
    return plane + beyond + sides + [place.up, place.down, place.sibling]


def exists(direction, dist, piece):
    return dist < 4 or (dist == 4 and piece == direction)


def step_kernel(
    t_ref, ident_ref, freqs, table, clip_hbm, target_hbm, proj_hbm, w1, w2, r1, r2, update, kept,
    clip, target, proj, same_group, act_one, act_two, err, grad_hid, flip_one, flip_two, hid, weights, grad,
    gbuf, rbuf, wbuf, blocks, sib_in, cross_out, cross_in, hop_out, hop_in, last_out, last_in, x_out, x_in, rate_rows,
    load_sem, gsend, grecv, rate_send, rate_recv, zsend, zrecv, ssend, srecv, bsend, brecv, tsend, trecv,
    rsend, rrecv, ysend, yrecv, psend, precv, csend, crecv,
):
    f32, bf16 = jnp.float32, jnp.bfloat16
    place = Place()
    sends = []

    def go(copy):
        copy.start()
        sends.append(copy)

    barrier = pltpu.get_barrier_semaphore()
    friends = partners(place)
    for friend in friends:
        pl.semaphore_signal(barrier, inc=1, device_id=friend, device_id_type=MESH)
    for index, ref in enumerate((w1, w2)):
        gbuf[index, 0, place.g] = ref[...]
    for index, ref in enumerate((r1, r2)):
        rbuf[index, place.g] = ref[...]
    first = lax.broadcasted_iota(jnp.int32, (C, C), 0)
    second = lax.broadcasted_iota(jnp.int32, (C, C), 1)
    same_group[...] = (((first * 3277) >> 16) == ((second * 3277) >> 16)).astype(f32).astype(bf16)
    blank = jnp.zeros((HW, C), bf16)
    for ref in (act_one, act_two, err, grad_hid):
        ref[0:HW, :] = blank
        ref[HW + POINTS :, :] = blank
    zero = jnp.zeros((8, C), f32)
    grad[TAPS:, :] = zero
    pl.semaphore_wait(barrier, len(friends))

    def group_copy(w, beyond, step, here):
        source = place.g if here else lax.rem(place.g + (N_GROUP - step), N_GROUP)
        to = (place.peer(step), place.opposite if beyond else place.m)
        at = (w, beyond, step)
        return remote(gbuf.at[w, 0, source if not beyond else place.g], gbuf.at[w, beyond, source],
                      gsend.at[at], grecv.at[at], to)

    def group_send(w):
        for beyond in range(2):
            for step in range(1 - beyond, N_GROUP):
                go(group_copy(w, beyond, step, True))

    def rate_copy(step, here):
        source = place.g if here else lax.rem(place.g + (N_GROUP - step), N_GROUP)
        ref = rbuf.at[:, source]
        return remote(ref, ref, rate_send.at[step], rate_recv.at[step], (place.peer(step), place.m))

    group_send(0)
    loads = [
        pltpu.make_async_copy(src, dst, load_sem.at[i])
        for i, (src, dst) in enumerate(((clip_hbm, clip), (proj_hbm, proj), (target_hbm, target)))
    ]
    loads[0].start()
    loads[1].start()

    def assemble(read):
        return jnp.concatenate([read(group).astype(f32) for group in range(N_GROUP)], axis=1)

    tile_slot = (2 * place.x_lo, 2 - 2 * place.x_lo, 1 + 2 * place.y_lo, 3 - 2 * place.y_lo)

    def slot(w, dist, piece, first, count):
        return wbuf.at[w, place.zof(-dist), place.core, place.xof(piece), pl.ds(first, count)]

    def slots(w, dist, first, count, core=None):
        core = place.core if core is None else core
        return wbuf.at[w, place.zof(-dist), core, :, pl.ds(first, count)]

    def share_copy(w, dist, high, count, here):
        ref = slots(w, dist, 2 * high, count, place.core if here else 1 - place.core)
        at = (w, high, dist % NZ)
        return remote(ref, ref, ssend.at[at], srecv.at[at], place.sibling)

    def side_copy(w, side, dist):
        src, dst = slots(w, dist, side, 1), slots(w, dist, side + 2, 1)
        at = (w, side, dist % NZ)
        return remote(src, dst, bsend.at[at], brecv.at[at], (place.beside_x, place.beside_y)[side])

    def ring_copy(w, direction, dist, piece, here):
        sign = 1 if direction == 0 else -1
        ref = slot(w, sign * (dist - 1 if here else dist), piece, 0, 2)
        to = place.up if direction == 0 else place.down
        return remote(ref, ref, zsend.at[w, direction, dist, piece], zrecv.at[w, direction, dist, piece], to)

    def forward(w, direction, dist, piece):
        if exists(direction, dist, piece):
            go(ring_copy(w, direction, dist, piece, True))

    def end_copy(w, side):
        src, dst = slots(w, 4, side, 1), slots(w, 4, side + 2, 1)
        to = ((place.beside_x, place.beside_y)[side][0], place.twin)
        return remote(src, dst, tsend.at[w, side], trecv.at[w, side], to)

    def end_in(w, side):
        ref = slots(w, 4, side + 2, 1, 1 - place.core)
        return remote(ref, ref, tsend.at[w, side], trecv.at[w, side], place.sibling)

    def hand_on(w, dist):
        for side in range(2):
            go(side_copy(w, side, dist))
            if dist == 4:
                go(end_copy(w, side))
        go(share_copy(w, dist, 0, 2, True))

    def plane_block(w, piece):
        for step in range(1 - piece, N_GROUP):
            group_copy(w, piece, step, False).wait_recv()
        rows_f32 = assemble(lambda group: gbuf[w, piece, group])
        whole = jnp.concatenate([rows_f32, jnp.zeros((4, C), f32)], axis=0).astype(bf16)
        if piece == 0:
            kept[w] = rows_f32
        for tile in range(4):
            wbuf[w, place.z, place.core, place.xof(piece), tile_slot[tile]] = whole[16 * tile : 16 * (tile + 1)]
        for direction in range(2):
            forward(w, direction, 1, piece)

    def ring_start(w):
        for piece in range(2):
            plane_block(w, piece)
        go(share_copy(w, 0, 0, 4, True))

    def ring_step(w, dist):
        for piece in range(2):
            for direction in range(2):
                if exists(direction, dist, piece):
                    ring_copy(w, direction, dist, piece, False).wait_recv()
                    forward(w, direction, dist + 1, piece)
        for far in sorted({dist, NZ - dist}):
            hand_on(w, far)

    def ring_sides(w, dist):
        for far in sorted({dist, NZ - dist}):
            for side in range(2):
                side_copy(w, side, far).wait_recv()
            if dist < 4:
                go(share_copy(w, far, 1, 2, True))

    def dense(w):
        for dist in range(NZ):
            share_copy(w, dist, 0, 2 if dist else 4, False).wait_recv()
            if dist == 4:
                for side in range(2):
                    end_in(w, side).wait_recv()
            elif dist:
                share_copy(w, dist, 1, 2, False).wait_recv()
        for m in range(N_MEMBER):
            for tile in range(4):
                start, size = ROWS * m + 16 * tile, min(16, ROWS - 16 * tile)
                block = wbuf[w, (m // 2) % NZ, m % 2, m // 16, tile_slot[tile]]
                weights[w, start : start + size, :] = block[0:size]

    def lay(w):
        for m in range(N_MEMBER):
            for part in range(2):
                start = ROWS * m + PART * part
                blocks[w, m // 16, (m // 2) % NZ, m % 2, part] = grad[start : start + PART, :]

    def pair_copy(w, dist, piece):
        src = blocks.at[w, place.xof(piece), place.zof(dist), 1 - place.core]
        dst = sib_in.at[w, dist, piece]
        return remote(src, dst, psend.at[w, dist, piece], precv.at[w, dist, piece], place.sibling)

    def pair(w):
        for dist in (4, 3, 5, 2, 6, 1, 7, 0):
            for piece in (1, 0):
                go(pair_copy(w, dist, piece))

    paired = set()

    def summed(w, dist, piece, part):
        if (w, dist, piece) not in paired:
            paired.add((w, dist, piece))
            pair_copy(w, dist, piece).wait_recv()
        return blocks[w, place.xof(piece), place.zof(dist), place.core, part] + sib_in[w, dist, piece, part]

    def cross_copy(w, dist):
        at = (w, dist)
        return remote(cross_out.at[at], cross_in.at[at], csend.at[at], crecv.at[at], place.across)

    def cross(w, *dists):
        for dist in dists:
            cross_out[w, dist] = summed(w, dist, 1, 0).astype(bf16)
            go(cross_copy(w, dist))

    def crossed(w, dist):
        cross_copy(w, dist).wait_recv()
        return summed(w, dist, 0, 0) + cross_in[w, dist].astype(f32)

    def hop(w, lane, direction, dist):
        at = (w, lane, direction, dist)
        to = place.up if direction == 0 else place.down
        if dist == 1:
            src, dst = last_out.at[w, direction, lane], last_in.at[w, direction, lane]
        else:
            src, dst = hop_out.at[w, direction, dist - 2, lane], hop_in.at[w, direction, dist - 2, lane]
        if lane == 2 and dist == 4:
            src, dst = src.at[pl.ds(16 * direction, 16)], dst.at[pl.ds(16 * direction, 16)]
        return src, dst, remote(src, dst, rsend.at[at], rrecv.at[at], to)

    def far(direction, dist):
        return dist if direction == 0 else NZ - dist

    def ring_z(w, dist):
        for piece in (1, 0):
            for direction in range(2):
                if not exists(direction, dist, piece):
                    continue
                total = summed(w, far(direction, dist), piece, 1)
                if exists(direction, dist + 1, piece):
                    _, arrived, copy = hop(w, piece, direction, dist + 1)
                    copy.wait_recv()
                    total = total + arrived[...].astype(f32)
                src, _, copy = hop(w, piece, direction, dist)
                src[...] = total.astype(src.dtype)
                go(copy)

    def ring_x(w, dist):
        own_sum = crossed(w, 4) if dist == 4 else None
        for direction in range(2):
            src, _, copy = hop(w, 2, direction, dist)
            if dist == 4:
                src[...] = own_sum[16 * direction : 16 * (direction + 1)].astype(src.dtype)
            else:
                _, arrived, before = hop(w, 2, direction, dist + 1)
                total = crossed(w, far(direction, dist))
                before.wait_recv()
                if dist == 3:
                    low, high = total[:16], total[16:]
                    if direction == 0:
                        low = low + arrived[...].astype(f32)
                    else:
                        high = high + arrived[...].astype(f32)
                    src[0:16] = low.astype(src.dtype)
                    src[16:PART] = high.astype(src.dtype)
                else:
                    src[...] = (total + arrived[...].astype(f32)).astype(src.dtype)
            go(copy)

    def last_hops(w, lane, total):
        for direction in range(2):
            _, arrived, copy = hop(w, lane, direction, 1)
            copy.wait_recv()
            total = total + arrived[...]
        return total

    def swap_copy(w):
        return remote(x_out.at[w], x_in.at[w], ysend.at[w], yrecv.at[w], place.across)

    def turn(w):
        x_out[w] = last_hops(w, 1, summed(w, 0, 1, 1))
        go(swap_copy(w))

    def finish(w):
        total = last_hops(w, 2, crossed(w, 0))
        update[w, 0:PART, :] = rate_rows[w, 0:PART, :] * total
        total = last_hops(w, 0, summed(w, 0, 0, 1))
        swap_copy(w).wait_recv()
        total = total + x_in[w]
        update[w, PART:ROWS, :] = rate_rows[w, PART:ROWS, :] * total[0 : ROWS - PART]

    def scatter(w):
        cross(w, 4, 3, 5)
        ring_z(w, 4)
        yield 1
        cross(w, 2, 6)
        yield 2
        ring_z(w, 3)
        yield 3
        ring_x(w, 4)
        cross(w, 1, 7, 0)
        yield 4
        ring_z(w, 2)
        ring_x(w, 3)
        yield 5
        ring_z(w, 1)
        ring_x(w, 2)
        yield 6
        turn(w)
        yield 7
        ring_x(w, 1)
        yield 8
        finish(w)
        yield 9

    def rows(index, size=UNIT):
        return pl.ds(index * size, size)

    def fold(values):
        return values.reshape(values.shape[0] // 8, 8, C).sum(axis=0)

    def spread(sums):
        column = sums.sum(axis=0, keepdims=True)
        top = column.astype(bf16)
        rest = column - top.astype(f32)
        middle = rest.astype(bf16)
        low = (rest - middle.astype(f32)).astype(bf16)
        terms = jnp.concatenate([top, middle, low, jnp.zeros((13, C), bf16)], axis=0)
        total = jnp.dot(terms, same_group[...], preferred_element_type=f32)
        return total.sum(axis=0, keepdims=True) * (1.0 / (POINTS * PER_GROUP))

    def sweep(body, start):
        return lax.fori_loop(0, FRAMES, lambda i, carry: body(pl.ds(pl.multiple_of(i * HW, HW), HW), carry), start)

    def padded(i):
        return pl.ds(HW + i * UNIT, UNIT)

    def silu(v):
        return v / (1.0 + jnp.exp(-v))

    loads[0].wait()
    centre = spread(sweep(lambda at, acc: acc + fold(clip[at, :].astype(f32)), zero))

    def squares(ref, mean):
        def body(at, acc):
            off = ref[at, :].astype(f32) - mean
            return acc + fold(off * off)

        return lax.rsqrt(spread(sweep(body, zero)) + 1e-05)

    inverse = squares(clip, centre)
    units = POINTS // UNIT

    def act_unit(i):
        values = (clip[rows(i), :].astype(f32) - centre) * inverse
        act_one[padded(i), :] = silu(values).astype(bf16)

    def flip_unit(flipped, ref, i):
        flipped[:, rows(i)] = ref[padded(i), :].T

    ring_start(0)
    group_send(1)
    loads[2].start()
    for i in range(4):
        act_unit(i)
    ring_step(0, 1)
    ring_start(1)
    act_unit(4)
    act_unit(5)
    ring_step(0, 2)
    ring_step(1, 1)
    act_unit(6)
    ring_sides(0, 1)
    loads[1].wait()
    half_width = freqs.shape[1]
    angles = t_ref[0].astype(f32) * freqs[...]
    person = table[pl.ds(ident_ref[0], 1), :]
    embedding = jnp.concatenate([jnp.cos(angles), jnp.sin(angles)], axis=1) + person
    embed = jnp.broadcast_to(silu(embedding).astype(bf16), (16, 2 * half_width))
    bias = jnp.dot(embed, proj[...], preferred_element_type=f32)[0:1]
    ring_step(0, 3)
    ring_step(1, 2)
    for i in range(3):
        flip_unit(flip_one, act_one, i)
    ring_sides(0, 2)
    ring_step(0, 4)
    ring_step(1, 3)
    ring_sides(1, 1)
    for i in range(3, units):
        flip_unit(flip_one, act_one, i)
    ring_sides(0, 3)
    ring_sides(0, 4)
    ring_step(1, 4)
    ring_sides(1, 2)
    dense(0)

    def stacked(ref, start, size, taps):
        return jnp.concatenate([ref[pl.ds(start + HW * tap, size), :] for tap in taps], axis=1)

    half = POINTS // 2
    sums = zero
    for part in range(2):
        mixed = jnp.dot(stacked(act_one, part * half, half, (0, 1, 2)), weights[0], preferred_element_type=f32)
        values = SCALE * mixed + bias
        hid[pl.ds(part * half, half), :] = values
        sums = sums + fold(values)
        ring_sides(1, 3 + part)
    for step in range(1, N_GROUP):
        go(rate_copy(step, True))
    centre_two = spread(sums)
    inverse_two = squares(hid, centre_two)
    for i in range(units):
        values = (hid[rows(i), :] - centre_two) * inverse_two
        hid[rows(i), :] = values
        act_two[padded(i), :] = silu(values).astype(bf16)
    for i in range(units):
        flip_unit(flip_two, act_two, i)
    dense(1)
    loads[2].wait()

    for part in range(2):
        at = pl.ds(part * half, half)
        mixed = jnp.dot(stacked(act_two, part * half, half, (0, 1, 2)), weights[1], preferred_element_type=f32)
        output = clip[at, :].astype(f32) + SCALE * mixed
        err[pl.ds(HW + part * half, half), :] = (output - target[at, :].astype(f32)).astype(bf16)

    def weight_grad(flipped, ref, tap):
        grad[C * tap : C * (tap + 1), :] = jnp.dot(
            flipped[...], ref[pl.ds(HW * (2 - tap), POINTS), :], preferred_element_type=f32
        )

    for tap in range(3):
        weight_grad(flip_two, err, tap)
    lay(1)
    pair(1)

    scatter_two = scatter(1)
    sum_grad, sum_mixed = zero, zero
    for part in range(2):
        at = pl.ds(part * half, half)
        back = jnp.zeros((half, C), f32)
        for tap in range(3):
            back = back + lax.dot_general(
                err[pl.ds(part * half + HW * (2 - tap), half), :],
                weights[1, C * tap : C * (tap + 1), :],
                (((1,), (1,)), ((), ())),
                preferred_element_type=f32,
            )
        values = hid[at, :]
        gate = 1.0 / (1.0 + jnp.exp(-values))
        inner = (SCALE * back) * (gate * (1.0 + values * (1.0 - gate)))
        grad[at, :] = inner
        sum_grad = sum_grad + fold(inner)
        sum_mixed = sum_mixed + fold(inner * values)
        next(scatter_two)
        if part:
            next(scatter_two)
    mean_grad, mean_mixed = spread(sum_grad), spread(sum_mixed)
    for i in range(units):
        inner = grad[rows(i), :] - mean_grad - hid[rows(i), :] * mean_mixed
        grad_hid[padded(i), :] = (inner * inverse_two).astype(bf16)
    next(scatter_two)
    for tap in range(3):
        weight_grad(flip_one, grad_hid, tap)
        if tap == 1:
            next(scatter_two)
    lay(0)
    pair(0)
    scatter_one = scatter(0)
    next(scatter_one)
    next(scatter_one)
    next(scatter_two)
    for _ in range(3):
        next(scatter_one)
    for step in range(1, N_GROUP):
        rate_copy(step, False).wait_recv()
    for w in range(2):
        rate_rows[w] = assemble(lambda group: rbuf[w, group]) * SCALE
    next(scatter_two)
    next(scatter_two)
    next(scatter_one)
    next(scatter_two)
    for _ in range(3):
        next(scatter_one)
    for copy in sends:
        copy.wait_send()


def step(timestep, identity, freqs, table, clip, target, time_proj, w1, w2, r1, r2):
    f32, bf16 = jnp.float32, jnp.bfloat16
    dma = pltpu.SemaphoreType.DMA
    vmem = pl.BlockSpec(memory_space=pltpu.VMEM)
    smem = pl.BlockSpec(memory_space=pltpu.SMEM)
    anywhere = pl.BlockSpec(memory_space=pl.ANY)
    part = (PART, C)
    wide = (POINTS + 2 * HW, C)
    rows = jax.ShapeDtypeStruct((2, ROWS, C), f32)
    return pl.pallas_call(
        step_kernel,
        out_shape=(rows, rows),
        in_specs=[smem] * 2 + [vmem] * 2 + [anywhere] * 3 + [vmem] * 4,
        out_specs=(vmem,) * 2,
        scratch_shapes=[
            pltpu.VMEM((POINTS, C), bf16),
            pltpu.VMEM((POINTS, C), bf16),
            pltpu.VMEM(time_proj.shape, bf16),
            pltpu.VMEM((C, C), bf16),
            pltpu.VMEM(wide, bf16),
            pltpu.VMEM(wide, bf16),
            pltpu.VMEM(wide, bf16),
            pltpu.VMEM(wide, bf16),
            pltpu.VMEM((C, POINTS), bf16),
            pltpu.VMEM((C, POINTS), bf16),
            pltpu.VMEM((POINTS, C), f32),
            pltpu.VMEM((2, TAPS, C), bf16),
            pltpu.VMEM((TAPS + 8, C), f32),
            pltpu.VMEM((2, NX, N_GROUP, ROWS, COLS), bf16),
            pltpu.VMEM((2, N_GROUP, ROWS, COLS), bf16),
            pltpu.VMEM((2, NZ, NC, NX, 4, 16, C), bf16),
            pltpu.VMEM((2, NX, NZ, NC, 2) + part, f32),
            pltpu.VMEM((2, NZ, 2, 2) + part, f32),
            pltpu.VMEM((2, NZ) + part, bf16),
            pltpu.VMEM((2, NZ) + part, bf16),
            pltpu.VMEM((2, 2, 3, 3) + part, bf16),
            pltpu.VMEM((2, 2, 3, 3) + part, bf16),
            pltpu.VMEM((2, 2, 3) + part, f32),
            pltpu.VMEM((2, 2, 3) + part, f32),
            pltpu.VMEM((2,) + part, f32),
            pltpu.VMEM((2,) + part, f32),
            pltpu.VMEM((2, ROWS, C), f32),
            dma((3,)),
            dma((2, 2, N_GROUP)),
            dma((2, 2, N_GROUP)),
            dma((N_GROUP,)),
            dma((N_GROUP,)),
            dma((2, 2, 5, 2)),
            dma((2, 2, 5, 2)),
            dma((2, 2, NZ)),
            dma((2, 2, NZ)),
            dma((2, 2, NZ)),
            dma((2, 2, NZ)),
            dma((2, 2)),
            dma((2, 2)),
            dma((2, 3, 2, 5)),
            dma((2, 3, 2, 5)),
            dma((2,)),
            dma((2,)),
            dma((2, NZ, 2)),
            dma((2, NZ, 2)),
            dma((2, NZ)),
            dma((2, NZ)),
        ],
        compiler_params=pltpu.CompilerParams(
            collective_id=0, has_side_effects=True, vmem_limit_bytes=62 << 20
        ),
        name="inner_step",
    )(timestep, identity, freqs, table, clip, target, time_proj, w1, w2, r1, r2)


def shards(
    clips,
    targets,
    timestep,
    identity,
    conv1_weight,
    conv2_weight,
    rate1,
    rate2,
    time_proj,
    subject_table,
):
    half_width = subject_table.shape[1] // 2
    freqs = np.exp(-math.log(10000.0) * np.arange(half_width) / half_width).astype(np.float32)
    update, kept = step(
        timestep,
        identity,
        freqs[None],
        subject_table,
        clips.reshape(POINTS, C),
        targets.reshape(POINTS, C),
        time_proj,
        conv1_weight,
        conv2_weight,
        rate1,
        rate2,
    )
    return tuple((kept[w] - update[w])[None] for w in range(2))


def solution(mesh):
    return jax.shard_map(
        shards,
        mesh=mesh,
        in_specs=(
            P(("group", "member"), None, None, None),
            P(("group", "member"), None, None, None),
            P(("group", "member")),
            P(("group", "member")),
            P("member", "group"),
            P("member", "group"),
            P("member", "group"),
            P("member", "group"),
            P(),
            P(),
        ),
        out_specs=(P("group", "member", None), P("group", "member", None)),
        check_vma=False,
    )
```

time: 100 us -> 99.2 us (level); the launches traced: 100 us -> 97.5 us
  Pallas kernels: 94.2 us -> 92.8 us
    pallas_call x1, Pallas kernels: 94.2 us -> 92.8 us  [step(): pl.pallas_call(step_kernel, out_shape=(rows, rows), in_specs=[smem] * 2 +...]
    sub x1, other arithmetic: 0.05 us -> 1.19 us  [shards(): return tuple(((kept[w] - update[w])[None] for w in range(2)))]
    convert_element_type x2 -> x0, other arithmetic: 1.08 us -> none  [the longest x1 1.06 us: shards(): own = own.astype(jnp.float32)]
where the time goes in v5:
time: 99.2 us; the launch traced here: 97.5 us
  Pallas kernels  92.8 us (94%)
  between operations  1.93 us (2%)
  local copies, waits for them, and re-layouts  1.64 us (2%)
  other arithmetic  1.19 us (1%)
    pallas_call x1, Pallas kernels, step(): pl.pallas_call(step_kernel, out_shape=(rows, rows), in_specs=[smem] * 2 +...  92.8 us

profile of v5, /device:TPU:8, one launch (start us, length us, event | category | flops | bytes accessed | tf_op | source)
XLA Modules:
  0.0 97.5 jit_solution(14561553696139467139)
XLA Ops:
  1.9 92.8 %inner_step.1 = (f32[2,60,640]{2,1,0:T(8,128)}, f32[2,60,640]{2,1,0:T(8,128)}) custom-call(s32[1]{0:T(128)S(6)} %copy.15.t_ref, s32[1]{0:T(128)S(6)} %copy.16.ident_ref, f32[1,640]{1,0:T(1,128)} %constant.2.clone.freqs, f32[64,1280]{1,0:T(8,128)} %table.1, bf16[896,640]{1,0:T(8,128)(2,1)} %bitcast.2, bf16[896,640]{1,0:T(8,128)(2,1)} %bitcast.3, ...), custom_call_target="tpu_custom_call" | custom-call | tf_op jit(solution)/shard_map/inner_step/pallas_call | solution.py:543
  94.7 1.2 %slice_subtract_fusion = (f32[1,60,640]{2,1,0:T(8,128)S(1)}, f32[1,60,640]{2,1,0:T(8,128)S(1)}) fusion(f32[2,60,640]{2,1,0:T(8,128)} %get-tuple-element.5, f32[2,60,640]{2,1,0:T(8,128)} %get-tuple-element.4), kind=kLoop, calls=%fused_computation | loop fusion | flops 76800 | bytes 921600 | tf_op jit(solution)/shard_map/sub | solution.py:632
  95.9 0.8 copy.14
  96.7 0.8 copy.13

commit v6 on v5

--- a/solution.py
+++ b/solution.py
@@ -74,7 +74,7 @@
 def step_kernel(
     t_ref, ident_ref, freqs, table, clip_hbm, target_hbm, proj_hbm, w1, w2, r1, r2, update, kept,
     clip, target, proj, same_group, act_one, act_two, err, grad_hid, flip_one, flip_two, hid, weights, grad,
-    gbuf, rbuf, wbuf, blocks, sib_in, cross_out, cross_in, hop_out, hop_in, last_out, last_in, x_out, x_in, rate_rows,
+    gbuf, rbuf, wbuf, blocks, sib_in, cross_out, cross_in, hop_out, hop_in, near_out, last_in, x_out, x_in, rate_rows,
     load_sem, gsend, grecv, rate_send, rate_recv, zsend, zrecv, ssend, srecv, bsend, brecv, tsend, trecv,
     rsend, rrecv, ysend, yrecv, psend, precv, csend, crecv,
 ):
@@ -85,6 +85,11 @@
     def go(copy):
         copy.start()
         sends.append(copy)
+
+    def settle(count):
+        for copy in sends[:count]:
+            copy.wait_send()
+        del sends[:count]
 
     barrier = pltpu.get_barrier_semaphore()
     friends = partners(place)
@@ -184,7 +189,7 @@
         rows_f32 = assemble(lambda group: gbuf[w, piece, group])
         whole = jnp.concatenate([rows_f32, jnp.zeros((4, C), f32)], axis=0).astype(bf16)
         if piece == 0:
-            kept[w] = rows_f32
+            kept[w, :, 0, :] = rows_f32
         for tile in range(4):
             wbuf[w, place.z, place.core, place.xof(piece), tile_slot[tile]] = whole[16 * tile : 16 * (tile + 1)]
         for direction in range(2):
@@ -225,29 +230,27 @@
                 block = wbuf[w, (m // 2) % NZ, m % 2, m // 16, tile_slot[tile]]
                 weights[w, start : start + size, :] = block[0:size]
 
-    def lay(w):
-        for m in range(N_MEMBER):
-            for part in range(2):
-                start = ROWS * m + PART * part
-                blocks[w, m // 16, (m // 2) % NZ, m % 2, part] = grad[start : start + PART, :]
-
-    def pair_copy(w, dist, piece):
-        src = blocks.at[w, place.xof(piece), place.zof(dist), 1 - place.core]
-        dst = sib_in.at[w, dist, piece]
-        return remote(src, dst, psend.at[w, dist, piece], precv.at[w, dist, piece], place.sibling)
-
-    def pair(w):
-        for dist in (4, 3, 5, 2, 6, 1, 7, 0):
-            for piece in (1, 0):
-                go(pair_copy(w, dist, piece))
+    def pair_copy(w, xh, z):
+        src = blocks.at[w, xh, z, 1 - place.core]
+        dst = sib_in.at[w, xh, z]
+        return remote(src, dst, psend.at[w, xh, z], precv.at[w, xh, z], place.sibling)
+
+    def pair(w, first, last):
+        for q in range(first, last):
+            for m in (2 * q, 2 * q + 1):
+                for part in range(2):
+                    start = ROWS * m + PART * part
+                    blocks[w, q // NZ, q % NZ, m % 2, part] = grad[start : start + PART, :]
+            go(pair_copy(w, q // NZ, q % NZ))
 
     paired = set()
 
     def summed(w, dist, piece, part):
+        at = (place.xof(piece), place.zof(dist))
         if (w, dist, piece) not in paired:
             paired.add((w, dist, piece))
-            pair_copy(w, dist, piece).wait_recv()
-        return blocks[w, place.xof(piece), place.zof(dist), place.core, part] + sib_in[w, dist, piece, part]
+            pair_copy(w, *at).wait_recv()
+        return blocks[w, at[0], at[1], place.core, part] + sib_in[w, at[0], at[1], part]
 
     def cross_copy(w, dist):
         at = (w, dist)
@@ -262,11 +265,17 @@
         cross_copy(w, dist).wait_recv()
         return summed(w, dist, 0, 0) + cross_in[w, dist].astype(f32)
 
+    def merges(lane, direction):
+        return lane < 2 and direction != lane
+
     def hop(w, lane, direction, dist):
         at = (w, lane, direction, dist)
         to = place.up if direction == 0 else place.down
         if dist == 1:
-            src, dst = last_out.at[w, direction, lane], last_in.at[w, direction, lane]
+            src = near_out.at[w, direction, lane] if merges(lane, direction) else hop_in.at[w, direction, 0, lane]
+            dst = last_in.at[w, direction, 0, lane]
+        elif dist == 0:
+            src, dst = near_out.at[w, direction, lane], last_in.at[w, direction, 1, lane]
         else:
             src, dst = hop_out.at[w, direction, dist - 2, lane], hop_in.at[w, direction, dist - 2, lane]
         if lane == 2 and dist == 4:
@@ -275,6 +284,27 @@
 
     def far(direction, dist):
         return dist if direction == 0 else NZ - dist
+
+    def near_z(w):
+        for piece in (1, 0):
+            src, _, copy = hop(w, piece, piece, 0)
+            src[...] = summed(w, far(piece, 1), piece, 1).astype(bf16)
+            go(copy)
+
+    def near_x(w):
+        for direction in range(2):
+            src, _, copy = hop(w, 2, direction, 0)
+            src[...] = crossed(w, far(direction, 1)).astype(bf16)
+            go(copy)
+
+    def pass_on(w, lane):
+        for direction in range(2):
+            _, arrived, before = hop(w, lane, direction, 2)
+            before.wait_recv()
+            src, _, copy = hop(w, lane, direction, 1)
+            if merges(lane, direction):
+                src[...] = (summed(w, far(direction, 1), lane, 1) + arrived[...].astype(f32)).astype(bf16)
+            go(copy)
 
     def ring_z(w, dist):
         for piece in (1, 0):
@@ -314,9 +344,10 @@
 
     def last_hops(w, lane, total):
         for direction in range(2):
-            _, arrived, copy = hop(w, lane, direction, 1)
-            copy.wait_recv()
-            total = total + arrived[...]
+            for dist in (1,) if merges(lane, direction) else (0, 1):
+                _, arrived, copy = hop(w, lane, direction, dist)
+                copy.wait_recv()
+                total = total + arrived[...].astype(f32)
         return total
 
     def swap_copy(w):
@@ -328,17 +359,18 @@
 
     def finish(w):
         total = last_hops(w, 2, crossed(w, 0))
-        update[w, 0:PART, :] = rate_rows[w, 0:PART, :] * total
+        update[w, 0:PART, 0, :] = rate_rows[w, 0:PART, :] * total
         total = last_hops(w, 0, summed(w, 0, 0, 1))
         swap_copy(w).wait_recv()
         total = total + x_in[w]
-        update[w, PART:ROWS, :] = rate_rows[w, PART:ROWS, :] * total[0 : ROWS - PART]
+        update[w, PART:ROWS, 0, :] = rate_rows[w, PART:ROWS, :] * total[0 : ROWS - PART]
 
     def scatter(w):
         cross(w, 4, 3, 5)
         ring_z(w, 4)
         yield 1
         cross(w, 2, 6)
+        near_z(w)
         yield 2
         ring_z(w, 3)
         yield 3
@@ -348,12 +380,14 @@
         ring_z(w, 2)
         ring_x(w, 3)
         yield 5
-        ring_z(w, 1)
+        near_x(w)
+        pass_on(w, 1)
+        pass_on(w, 0)
         ring_x(w, 2)
         yield 6
         turn(w)
         yield 7
-        ring_x(w, 1)
+        pass_on(w, 2)
         yield 8
         finish(w)
         yield 9
@@ -474,10 +508,10 @@
             flipped[...], ref[pl.ds(HW * (2 - tap), POINTS), :], preferred_element_type=f32
         )
 
+    ready = (0, 5, 10, 16)
     for tap in range(3):
         weight_grad(flip_two, err, tap)
-    lay(1)
-    pair(1)
+        pair(1, ready[tap], ready[tap + 1])
 
     scatter_two = scatter(1)
     sum_grad, sum_mixed = zero, zero
@@ -507,28 +541,37 @@
     next(scatter_two)
     for tap in range(3):
         weight_grad(flip_one, grad_hid, tap)
+        pair(0, ready[tap], ready[tap + 1])
         if tap == 1:
             next(scatter_two)
-    lay(0)
-    pair(0)
     scatter_one = scatter(0)
-    next(scatter_one)
-    next(scatter_one)
+    early = 28
+    next(scatter_one)
+    next(scatter_one)
+    settle(early)
     next(scatter_two)
-    for _ in range(3):
-        next(scatter_one)
+    settle(early)
+    next(scatter_one)
+    settle(early)
+    next(scatter_one)
     for step in range(1, N_GROUP):
         rate_copy(step, False).wait_recv()
     for w in range(2):
         rate_rows[w] = assemble(lambda group: rbuf[w, group]) * SCALE
+    next(scatter_one)
+    settle(early)
     next(scatter_two)
     next(scatter_two)
+    settle(early)
     next(scatter_one)
     next(scatter_two)
-    for _ in range(3):
-        next(scatter_one)
-    for copy in sends:
-        copy.wait_send()
+    settle(early)
+    next(scatter_one)
+    settle(early)
+    next(scatter_one)
+    settle(early // 2)
+    next(scatter_one)
+    settle(len(sends))
 
 
 def step(timestep, identity, freqs, table, clip, target, time_proj, w1, w2, r1, r2):
@@ -539,7 +582,7 @@
     anywhere = pl.BlockSpec(memory_space=pl.ANY)
     part = (PART, C)
     wide = (POINTS + 2 * HW, C)
-    rows = jax.ShapeDtypeStruct((2, ROWS, C), f32)
+    rows = jax.ShapeDtypeStruct((2, ROWS, 1, C), f32)
     return pl.pallas_call(
         step_kernel,
         out_shape=(rows, rows),
@@ -563,13 +606,13 @@
             pltpu.VMEM((2, N_GROUP, ROWS, COLS), bf16),
             pltpu.VMEM((2, NZ, NC, NX, 4, 16, C), bf16),
             pltpu.VMEM((2, NX, NZ, NC, 2) + part, f32),
-            pltpu.VMEM((2, NZ, 2, 2) + part, f32),
+            pltpu.VMEM((2, NX, NZ, 2) + part, f32),
             pltpu.VMEM((2, NZ) + part, bf16),
             pltpu.VMEM((2, NZ) + part, bf16),
             pltpu.VMEM((2, 2, 3, 3) + part, bf16),
             pltpu.VMEM((2, 2, 3, 3) + part, bf16),
-            pltpu.VMEM((2, 2, 3) + part, f32),
-            pltpu.VMEM((2, 2, 3) + part, f32),
+            pltpu.VMEM((2, 2, 3) + part, bf16),
+            pltpu.VMEM((2, 2, 2, 3) + part, bf16),
             pltpu.VMEM((2,) + part, f32),
             pltpu.VMEM((2,) + part, f32),
             pltpu.VMEM((2, ROWS, C), f32),
@@ -590,8 +633,8 @@
             dma((2, 3, 2, 5)),
             dma((2,)),
             dma((2,)),
-            dma((2, NZ, 2)),
-            dma((2, NZ, 2)),
+            dma((2, NX, NZ)),
+            dma((2, NX, NZ)),
             dma((2, NZ)),
             dma((2, NZ)),
         ],
@@ -629,7 +672,7 @@
         rate1,
         rate2,
     )
-    return tuple((kept[w] - update[w])[None] for w in range(2))
+    return tuple((kept[w] - update[w]).transpose(1, 0, 2) for w in range(2))
 
 
 def solution(mesh):

time: 99.2 us -> 94.9 us (0.957)
  Pallas kernels: 92.8 us -> 89.6 us
  local copies, waits for them, and re-layouts: 1.64 us -> 0 us
    pallas_call x1, Pallas kernels: 92.8 us -> 89.6 us  [step(): pl.pallas_call(step_kernel, out_shape=(rows, rows), in_specs=[smem] * 2 +...]
    unnamed x2 -> x0, local copies, waits for them, and re-layouts: 1.64 us -> none
where the time goes in v6:
time: 94.9 us; the launch traced here: 93.7 us
  Pallas kernels  89.6 us (94%)
  other arithmetic  2.17 us (2%)
  between operations  1.93 us (2%)
    pallas_call x1, Pallas kernels, step(): pl.pallas_call(step_kernel, out_shape=(rows, rows), in_specs=[smem] * 2 +...  89.6 us
    sub x1, other arithmetic, shards(): return tuple(((kept[w] - update[w]).transpose(1, 0, 2) for w in range(2)))  2.17 us

profile of v6, /device:TPU:8, one launch (start us, length us, event | category | flops | bytes accessed | tf_op | source)
XLA Modules:
  0.0 93.7 jit_solution(10721041614616109444)
XLA Ops:
  1.9 89.6 %inner_step.1 = (f32[2,60,1,640]{3,2,1,0:T(1,128)}, f32[2,60,1,640]{3,2,1,0:T(1,128)}) custom-call(s32[1]{0:T(128)S(6)} %copy.13.t_ref, s32[1]{0:T(128)S(6)} %copy.14.ident_ref, f32[1,640]{1,0:T(1,128)} %constant.2.clone.freqs, f32[64,1280]{1,0:T(8,128)} %table.1, bf16[896,640]{1,0:T(8,128)(2,1)} %bitcast.6, bf16[896,640]{1,0:T(8,128)(2,1)} %bitcast.7, ...), custom_call_target="tpu_custom_call" | custom-call | tf_op jit(solution)/shard_map/inner_step/pallas_call | solution.py:586
  91.5 2.2 %subtract_bitcast_fusion = (f32[1,60,640]{2,0,1:T(1,128)}, f32[1,60,640]{2,0,1:T(1,128)}) fusion(f32[2,60,1,640]{3,2,1,0:T(1,128)} %get-tuple-element.5, f32[2,60,1,640]{3,2,1,0:T(1,128)} %get-tuple-element.4), kind=kLoop, calls=%fused_computation | loop fusion | flops 76800 | bytes 921600 | tf_op jit(solution)/shard_map/sub | solution.py:675

commit v7 on v6

--- a/solution.py
+++ b/solution.py
@@ -19,7 +19,8 @@
 PER_GROUP = C // GN_GROUPS
 SCALE = 1.0 / math.sqrt(TAPS)
 UNIT = 128
-PART = 32
+PADDED = 64
+CROSSED = (48, 32)
 
 
 class Place:
@@ -238,9 +239,7 @@
     def pair(w, first, last):
         for q in range(first, last):
             for m in (2 * q, 2 * q + 1):
-                for part in range(2):
-                    start = ROWS * m + PART * part
-                    blocks[w, q // NZ, q % NZ, m % 2, part] = grad[start : start + PART, :]
+                blocks[w, q // NZ, q % NZ, m % 2] = grad[ROWS * m : ROWS * m + PADDED, :]
             go(pair_copy(w, q // NZ, q % NZ))
 
     paired = set()
@@ -250,20 +249,24 @@
         if (w, dist, piece) not in paired:
             paired.add((w, dist, piece))
             pair_copy(w, *at).wait_recv()
-        return blocks[w, at[0], at[1], place.core, part] + sib_in[w, at[0], at[1], part]
+        part_rows = pl.ds(0, CROSSED[w]) if part == 0 else pl.ds(CROSSED[w], PADDED - CROSSED[w])
+        return blocks[w, at[0], at[1], place.core, part_rows] + sib_in[w, at[0], at[1], part_rows]
 
     def cross_copy(w, dist):
-        at = (w, dist)
-        return remote(cross_out.at[at], cross_in.at[at], csend.at[at], crecv.at[at], place.across)
+        at, span = (w, dist), pl.ds(0, CROSSED[w])
+        return remote(cross_out.at[at].at[span], cross_in.at[at].at[span], csend.at[at], crecv.at[at], place.across)
 
     def cross(w, *dists):
         for dist in dists:
-            cross_out[w, dist] = summed(w, dist, 1, 0).astype(bf16)
+            cross_out[w, dist, 0 : CROSSED[w]] = summed(w, dist, 1, 0).astype(bf16)
             go(cross_copy(w, dist))
 
     def crossed(w, dist):
         cross_copy(w, dist).wait_recv()
-        return summed(w, dist, 0, 0) + cross_in[w, dist].astype(f32)
+        return summed(w, dist, 0, 0) + cross_in[w, dist, 0 : CROSSED[w]].astype(f32)
+
+    def middle(w):
+        return (CROSSED[w] // 2 + 15) // 16 * 16
 
     def merges(lane, direction):
         return lane < 2 and direction != lane
@@ -278,8 +281,13 @@
             src, dst = near_out.at[w, direction, lane], last_in.at[w, direction, 1, lane]
         else:
             src, dst = hop_out.at[w, direction, dist - 2, lane], hop_in.at[w, direction, dist - 2, lane]
-        if lane == 2 and dist == 4:
-            src, dst = src.at[pl.ds(16 * direction, 16)], dst.at[pl.ds(16 * direction, 16)]
+        if lane < 2:
+            span = pl.ds(0, PADDED - CROSSED[w])
+        elif dist == 4:
+            span = pl.ds(0, middle(w)) if direction == 0 else pl.ds(middle(w), CROSSED[w] - middle(w))
+        else:
+            span = pl.ds(0, CROSSED[w])
+        src, dst = src.at[span], dst.at[span]
         return src, dst, remote(src, dst, rsend.at[at], rrecv.at[at], to)
 
     def far(direction, dist):
@@ -325,19 +333,19 @@
         for direction in range(2):
             src, _, copy = hop(w, 2, direction, dist)
             if dist == 4:
-                src[...] = own_sum[16 * direction : 16 * (direction + 1)].astype(src.dtype)
+                src[...] = (own_sum[: middle(w)] if direction == 0 else own_sum[middle(w) :]).astype(src.dtype)
             else:
                 _, arrived, before = hop(w, 2, direction, dist + 1)
                 total = crossed(w, far(direction, dist))
                 before.wait_recv()
                 if dist == 3:
-                    low, high = total[:16], total[16:]
+                    low, high = total[: middle(w)], total[middle(w) :]
                     if direction == 0:
                         low = low + arrived[...].astype(f32)
                     else:
                         high = high + arrived[...].astype(f32)
-                    src[0:16] = low.astype(src.dtype)
-                    src[16:PART] = high.astype(src.dtype)
+                    src[0 : middle(w)] = low.astype(src.dtype)
+                    src[middle(w) : CROSSED[w]] = high.astype(src.dtype)
                 else:
                     src[...] = (total + arrived[...].astype(f32)).astype(src.dtype)
             go(copy)
@@ -351,19 +359,21 @@
         return total
 
     def swap_copy(w):
-        return remote(x_out.at[w], x_in.at[w], ysend.at[w], yrecv.at[w], place.across)
+        span = pl.ds(0, PADDED - CROSSED[w])
+        return remote(x_out.at[w].at[span], x_in.at[w].at[span], ysend.at[w], yrecv.at[w], place.across)
 
     def turn(w):
-        x_out[w] = last_hops(w, 1, summed(w, 0, 1, 1))
+        x_out[w, 0 : PADDED - CROSSED[w]] = last_hops(w, 1, summed(w, 0, 1, 1))
         go(swap_copy(w))
 
     def finish(w):
         total = last_hops(w, 2, crossed(w, 0))
-        update[w, 0:PART, 0, :] = rate_rows[w, 0:PART, :] * total
+        cut = CROSSED[w]
+        update[w, 0:cut, 0, :] = rate_rows[w, 0:cut, :] * total
         total = last_hops(w, 0, summed(w, 0, 0, 1))
         swap_copy(w).wait_recv()
-        total = total + x_in[w]
-        update[w, PART:ROWS, 0, :] = rate_rows[w, PART:ROWS, :] * total[0 : ROWS - PART]
+        total = total + x_in[w, 0 : PADDED - cut]
+        update[w, cut:ROWS, 0, :] = rate_rows[w, cut:ROWS, :] * total[0 : ROWS - cut]
 
     def scatter(w):
         cross(w, 4, 3, 5)
@@ -580,7 +590,7 @@
     vmem = pl.BlockSpec(memory_space=pltpu.VMEM)
     smem = pl.BlockSpec(memory_space=pltpu.SMEM)
     anywhere = pl.BlockSpec(memory_space=pl.ANY)
-    part = (PART, C)
+    part = (max(CROSSED), C)
     wide = (POINTS + 2 * HW, C)
     rows = jax.ShapeDtypeStruct((2, ROWS, 1, C), f32)
     return pl.pallas_call(
@@ -605,8 +615,8 @@
             pltpu.VMEM((2, NX, N_GROUP, ROWS, COLS), bf16),
             pltpu.VMEM((2, N_GROUP, ROWS, COLS), bf16),
             pltpu.VMEM((2, NZ, NC, NX, 4, 16, C), bf16),
-            pltpu.VMEM((2, NX, NZ, NC, 2) + part, f32),
-            pltpu.VMEM((2, NX, NZ, 2) + part, f32),
+            pltpu.VMEM((2, NX, NZ, NC, PADDED, C), f32),
+            pltpu.VMEM((2, NX, NZ, PADDED, C), f32),
             pltpu.VMEM((2, NZ) + part, bf16),
             pltpu.VMEM((2, NZ) + part, bf16),
             pltpu.VMEM((2, 2, 3, 3) + part, bf16),

time: 94.9 us -> 93.9 us (0.989)
  no operation moved by 1% of the time
where the time goes in v7:
time: 93.9 us; the launch traced here: 93.1 us
  Pallas kernels  89 us (95%)
  other arithmetic  2.17 us (2%)
  between operations  1.93 us (2%)
    pallas_call x1, Pallas kernels, step(): pl.pallas_call(step_kernel, out_shape=(rows, rows), in_specs=[smem] * 2 +...  89 us
    sub x1, other arithmetic, shards(): return tuple(((kept[w] - update[w]).transpose(1, 0, 2) for w in range(2)))  2.17 us

profile of v7, /device:TPU:8, one launch (start us, length us, event | category | flops | bytes accessed | tf_op | source)
XLA Modules:
  0.0 93.1 jit_solution(14730307650153508418)
XLA Ops:
  1.9 89.0 %inner_step.1 = (f32[2,60,1,640]{3,2,1,0:T(1,128)}, f32[2,60,1,640]{3,2,1,0:T(1,128)}) custom-call(s32[1]{0:T(128)S(6)} %copy.13.t_ref, s32[1]{0:T(128)S(6)} %copy.14.ident_ref, f32[1,640]{1,0:T(1,128)} %constant.2.clone.freqs, f32[64,1280]{1,0:T(8,128)} %table.1, bf16[896,640]{1,0:T(8,128)(2,1)} %bitcast.6, bf16[896,640]{1,0:T(8,128)(2,1)} %bitcast.7, ...), custom_call_target="tpu_custom_call" | custom-call | tf_op jit(solution)/shard_map/inner_step/pallas_call | solution.py:596
  90.9 2.2 %subtract_bitcast_fusion = (f32[1,60,640]{2,0,1:T(1,128)}, f32[1,60,640]{2,0,1:T(1,128)}) fusion(f32[2,60,1,640]{3,2,1,0:T(1,128)} %get-tuple-element.5, f32[2,60,1,640]{3,2,1,0:T(1,128)} %get-tuple-element.4), kind=kLoop, calls=%fused_computation | loop fusion | flops 76800 | bytes 921600 | tf_op jit(solution)/shard_map/sub | solution.py:685
